TPU v7x, 1024 devices: a whole 8x8x8 slice. The times are simulated.
1024 devices in a mesh: blk: 256 (over x, y, z_hi), head: 4 (over z_lo, core).
Axes of the slice: x: 8, y: 8, z: 8 (z_hi: 4, z_lo: 2; z = z_hi * 2 + z_lo), core: 2. Of those that a mesh axis runs over, the one named last changes fastest.
Arguments:
- queries: bfloat16 [131072, 2048], P(('blk', 'head')), may hold values from -8 to 8
- key_feats: bfloat16 [131072, 2048], P(('blk', 'head')), may hold values from -8 to 8
- value_feats: bfloat16 [131072, 2048], P(('blk', 'head')), may hold values from -6 to 6
- segment_ids: int32 [131072], P(('blk', 'head')), may hold values from 0 to 511, never falling along the last dimension, each value on 1 to 512 neighbouring positions
Outputs:
- attended: bfloat16 [131072, 2048], P(('blk', 'head'))
Inputs may be any that keep to these rules, and one draw needn't show every extreme that they name: `segment_ids`: ids never fall along the stream; every id from 0 to 511 names 1 to 512 consecutive tokens, and some document has exactly 512 tokens.
All inputs are finite; a program needn't handle non-finite values.
Results may differ from a plain program's by a relative error of at most 0.0044.
Values may be sent and summed in bfloat16 or wider, within the bound.
No kernel may reach another device: no remote copies, remote signals or barrier semaphores. Data moves between devices by JAX's collectives and lax.ppermute only.
A program may use at most 64 MiB of HBM per device.

v0:
```python
import functools
import math

import jax
import jax.numpy as jnp
from jax import lax
from jax.experimental import pallas as pl
from jax.experimental.pallas import tpu as pltpu
from jax.sharding import PartitionSpec as P


HD = 128
AXES = ("blk", "head")
NEG = -1e30
VMEM_LIMIT = 16 << 20
F32 = jnp.float32
BF16 = jnp.bfloat16


def pack_half(k_ref, v_ref, ids_ref, out_ref):
    tokens = k_ref.shape[0]
    heads = k_ref.shape[1] // HD
    full = heads * tokens
    for head in range(heads):
        cols = slice(head * HD, (head + 1) * HD)
        rows = head * tokens
        out_ref[rows : rows + tokens, :] = k_ref[:, cols]
        out_ref[full + rows : full + rows + tokens, :] = v_ref[:, cols].T
    ids = ids_ref[...] + 1
    row = lax.broadcasted_iota(jnp.int32, (16, tokens), 0)
    tile = jnp.where(row == 0, ids >> 4, jnp.where(row == 1, ids & 15, 0)).astype(F32).astype(BF16)
    out_ref[2 * full : 2 * full + 16, :] = tile


def pack_mine_kernel(core_ref, k_ref, v_ref, ids_ref, kv_out):
    pack_half(k_ref, v_ref, ids_ref, kv_out)


def pack_other_kernel(core_ref, k_ref, v_ref, q_other, q_mine, ids_ref, kvq_out, q_out):
    pack_half(k_ref, v_ref, ids_ref, kvq_out)
    tokens = k_ref.shape[0]
    heads = k_ref.shape[1] // HD
    at = 2 * heads * tokens + 16
    for head in range(heads):
        cols = slice(head * HD, (head + 1) * HD)
        rows = head * tokens
        kvq_out[at + rows : at + rows + tokens, :] = q_other[:, cols]
        q_out[rows : rows + tokens, :] = q_mine[:, cols]


def pack(core, queries, keys, values, ids):
    tokens, width = queries.shape
    half = width // 2
    heads = half // HD
    mine = pl.BlockSpec((tokens, half), lambda i, c: (0, c[0]))
    other = pl.BlockSpec((tokens, half), lambda i, c: (0, 1 - c[0]))
    id_spec = pl.BlockSpec((1, tokens), lambda i, c: (0, 0))
    rows = heads * tokens

    def whole(n):
        return pl.BlockSpec((n, HD), lambda i, c: (0, 0))

    def call(kernel, in_specs, sizes, *args):
        return pl.pallas_call(
            kernel,
            grid_spec=pltpu.PrefetchScalarGridSpec(
                num_scalar_prefetch=1, grid=(1,), in_specs=in_specs, out_specs=[whole(n) for n in sizes]
            ),
            out_shape=[jax.ShapeDtypeStruct((n, HD), BF16) for n in sizes],
            compiler_params=pltpu.CompilerParams(vmem_limit_bytes=VMEM_LIMIT),
        )(core, *args)

    (kv,) = call(pack_mine_kernel, [mine, mine, id_spec], [2 * rows + 16], keys, values, ids)
    keys, values, queries, kv = lax.optimization_barrier((keys, values, queries, kv))
    kvq, q = call(
        pack_other_kernel,
        [other, other, other, mine, id_spec],
        [3 * rows + 16, rows],
        keys,
        values,
        queries,
        queries,
        ids,
    )
    return kv, kvq, q


def id_row(ref, at):
    tile = ref[at : at + 16, :].astype(F32)
    return tile[0:1, :] * 16.0 + tile[1:2, :]


def attend_kernel(heads, tokens, groups, n_buf, first, last, *refs):
    refs = list(refs)
    qs = [refs.pop(0) for _ in range(groups)]
    qids = [refs.pop(0) for _ in range(groups)]
    bufs = [refs.pop(0) for _ in range(n_buf)]
    carry = [] if first else [(refs.pop(0), refs.pop(0)) for _ in range(groups)]
    if last:
        outs = [refs.pop(0) for _ in range(groups)]
    else:
        outs = [(refs.pop(0), refs.pop(0)) for _ in range(groups)]
    bias = refs.pop(0)
    full = heads * tokens
    at = 2 * full
    scale = 1.0 / (math.sqrt(HD) * math.log(2.0))
    query_ids = jnp.concatenate([id_row(q, at) for q in qids], axis=1)
    for b in range(n_buf):
        column = jnp.broadcast_to(id_row(bufs[b], at), (tokens, tokens)).T
        column = jnp.concatenate([column] * groups, axis=1)
        bias[b * tokens : (b + 1) * tokens, :] = jnp.where(column == query_ids, 0.0, NEG)
    q_base = [0 if q.shape[0] == full else 2 * full + 16 for q in qs]
    for head in range(heads):
        rows = slice(head * tokens, (head + 1) * tokens)
        v_rows = slice(full + head * tokens, full + (head + 1) * tokens)
        keys = jnp.concatenate([b[rows, :] for b in bufs], axis=0)
        vals = jnp.concatenate([b[v_rows, :] for b in bufs], axis=1)
        query = jnp.concatenate(
            [q[base + head * tokens : base + (head + 1) * tokens, :] for q, base in zip(qs, q_base)], axis=0
        )
        s = lax.dot_general(keys, query, (((1,), (1,)), ((), ())), preferred_element_type=F32)
        s = s * scale + bias[...]
        m = jnp.max(s, axis=0, keepdims=True)
        if not first:
            old_m = jnp.concatenate([stat[head : head + 1, :] for _, stat in carry], axis=1)
            old_l = jnp.concatenate([stat[heads + head : heads + head + 1, :] for _, stat in carry], axis=1)
            old_acc = jnp.concatenate([acc[rows, :] for acc, _ in carry], axis=1)
            m = jnp.maximum(m, old_m)
            alpha = jnp.exp2(old_m - m)
        p = jnp.exp2(s - m)
        l = jnp.sum(p, axis=0, keepdims=True)
        acc = jnp.dot(vals, p.astype(BF16), preferred_element_type=F32)
        if not first:
            l = l + alpha * old_l
            acc = acc + alpha * old_acc
        if last:
            acc = acc * (1.0 / l)
        for g in range(groups):
            lanes = slice(g * tokens, (g + 1) * tokens)
            if last:
                outs[g][rows, :] = acc[:, lanes].T.astype(BF16)
            else:
                new_acc, new_stat = outs[g]
                new_acc[rows, :] = acc[:, lanes]
                new_stat[head : head + 1, :] = m[:, lanes]
                new_stat[heads + head : heads + head + 1, :] = l[:, lanes]


def attend(heads, qs, qids, bufs, carry, last):
    groups, n_buf, tokens = len(qs), len(bufs), HD
    rows = heads * tokens
    first = not carry
    flat_carry = [x for pair in carry for x in pair]
    if last:
        shapes = [jax.ShapeDtypeStruct((rows, HD), BF16) for _ in range(groups)]
    else:
        shapes = [jax.ShapeDtypeStruct((n, tokens), F32) for _ in range(groups) for n in (rows, 2 * heads)]
    vmem = pl.BlockSpec(memory_space=pltpu.VMEM)
    elements = groups * rows * n_buf * tokens
    out = pl.pallas_call(
        functools.partial(attend_kernel, heads, tokens, groups, n_buf, first, last),
        in_specs=[vmem] * (2 * groups + n_buf + len(flat_carry)),
        out_specs=[vmem] * len(shapes),
        out_shape=shapes,
        scratch_shapes=[pltpu.VMEM((n_buf * tokens, groups * tokens), F32)],
        cost_estimate=pl.CostEstimate(
            flops=elements * 512, bytes_accessed=n_buf * rows * 512 + groups * rows * 1024, transcendentals=elements
        ),
        compiler_params=pltpu.CompilerParams(vmem_limit_bytes=VMEM_LIMIT),
    )(*qs, *qids, *bufs, *flat_carry)
    if last:
        return out
    return [(out[2 * g], out[2 * g + 1]) for g in range(groups)]


def place_kernel(core_ref, o_mine, o_back, out_ref):
    tokens = out_ref.shape[0]
    half = out_ref.shape[1] // 2
    heads = half // HD
    core = core_ref[0]
    for side in range(2):
        @pl.when(core == side)
        def _():
            for head in range(heads):
                rows = slice(head * tokens, (head + 1) * tokens)
                a = side * half + head * HD
                b = (1 - side) * half + head * HD
                out_ref[:, a : a + HD] = o_mine[rows, :]
                out_ref[:, b : b + HD] = o_back[rows, :]


def place(core, o_mine, o_back, tokens, width):
    vmem = pl.BlockSpec(memory_space=pltpu.VMEM)
    return pl.pallas_call(
        place_kernel,
        in_specs=[pl.BlockSpec(memory_space=pltpu.SMEM), vmem, vmem],
        out_specs=vmem,
        out_shape=jax.ShapeDtypeStruct((tokens, width), BF16),
        compiler_params=pltpu.CompilerParams(vmem_limit_bytes=VMEM_LIMIT),
        name="place",
    )(core, o_mine, o_back)


def layer(queries, key_feats, value_feats, segment_ids):
    count = lax.axis_size(AXES)
    tokens, width = queries.shape
    core = lax.axis_index("head") % 2
    core_arr = core.reshape(1).astype(jnp.int32)

    def shift(x, steps):
        return lax.ppermute(x, AXES, [(d, (d + steps) % count) for d in range(count)])

    def swap(x):
        return lax.ppermute(x, AXES, [(d, d ^ 1) for d in range(count)])

    kv, kvq, q = pack(core_arr, queries, key_feats, value_feats, segment_ids.reshape(1, tokens))
    up1 = shift(kv, 2)
    down1 = shift(kv, -2)
    kvq2 = swap(kvq)
    kv2 = kvq2[: kv.shape[0]]
    up1b = shift(kv2, 2)
    down1b = shift(kv2, -2)
    heads = width // 2 // HD
    qs, qids = [q, kvq2], [kv, kv2]
    carry = attend(heads, qs, qids, [kv, kv2], [], False)
    up1, down1, carry = lax.optimization_barrier((up1, down1, carry))
    up2 = shift(up1, 2)
    down2 = shift(down1, -2)
    carry = attend(heads, qs, qids, [up1, down1], carry, False)
    up1b, down1b, carry = lax.optimization_barrier((up1b, down1b, carry))
    up2b = shift(up1b, 2)
    down2b = shift(down1b, -2)
    carry = attend(heads, qs, qids, [up1b, down1b, up2, down2], carry, False)
    (o_other,) = attend(heads, [kvq2], [kv2], [up2b, down2b], [carry[1]], True)
    back = swap(o_other)
    (o_mine,) = attend(heads, [q], [kv], [up2b, down2b], [carry[0]], True)
    return place(core_arr, o_mine, back, tokens, width)


def solution(mesh):
    return jax.shard_map(
        layer,
        mesh=mesh,
        in_specs=(
            P(("blk", "head"), None),
            P(("blk", "head"), None),
            P(("blk", "head"), None),
            P(("blk", "head")),
        ),
        out_specs=P(("blk", "head"), None),
        check_vma=False,
    )
```

profile of v0, /device:TPU:1, one launch (start us, length us, event | category | flops | bytes accessed | tf_op | source)
XLA Modules:
  0.0 86.8 jit_solution(5036086043385882607)
XLA Ops:
  0.0 0.0 copy-start.3
  0.0 0.7 copy-done.3
  0.7 0.0 copy-start
  0.7 1.0 %copy-done = bf16[128,2048]{1,0:T(8,128)(2,1)S(1)} copy-done((bf16[128,2048]{1,0:T(8,128)(2,1)S(1)}, bf16[128,2048]{1,0:T(8,128)(2,1)}, u32[]{:S(2)}) %copy-start) | copy-done | bytes 524312
  1.7 0.0 copy-start.1
  1.7 1.0 %copy-done.1 = bf16[128,2048]{1,0:T(8,128)(2,1)S(1)} copy-done((bf16[128,2048]{1,0:T(8,128)(2,1)S(1)}, bf16[128,2048]{1,0:T(8,128)(2,1)}, u32[]{:S(2)}) %copy-start.1) | copy-done | bytes 524312
  2.7 0.0 copy-start.2
  2.7 0.2 shard_map.46.refs_2_.refs_4_.refs_1_
  2.9 0.8 copy-done.2
  3.8 0.3 shard_map.47
  4.0 16.0 %collective-permute-start = (bf16[3088,128]{1,0:T(8,128)(2,1)S(1)}, bf16[3088,128]{1,0:T(8,128)(2,1)S(1)}, u32[]{:S(2)}, u32[]{:S(2)}) collective-permute-start(bf16[3088,128]{1,0:T(8,128)(2,1)S(1)} %get-tuple-element.40), channel_id=1, source_target_pairs={{0,1},{1,0},{2,3},{3,2},{4,5},{5,4},{6,7},{7,6},{8,9},{9,8},{10,11... | collective-permute-start | bytes 2371592 | tf_op jit(solution)/shard_map/ppermute | solution.py:214
  20.1 1.9 %collective-permute-start.3 = (bf16[2064,128]{1,0:T(8,128)(2,1)S(1)}, bf16[2064,128]{1,0:T(8,128)(2,1)S(1)}, u32[]{:S(2)}, u32[]{:S(2)}) collective-permute-start(bf16[2064,128]{1,0:T(8,128)(2,1)S(1)} %shard_map.46.refs_2_.refs_4_.refs_1_), channel_id=1, source_target_pairs={{0,2},{1,3},{2,4},{3,5},{4,6},{5,7},{6,8},{7,9},{8,10},{9,11},{10,... | collective-permute-start | bytes 1585160 | tf_op jit(solution)/shard_map/ppermute | solution.py:211
  22.0 10.4 %collective-permute-start.4 = (bf16[2064,128]{1,0:T(8,128)(2,1)S(1)}, bf16[2064,128]{1,0:T(8,128)(2,1)S(1)}, u32[]{:S(2)}, u32[]{:S(2)}) collective-permute-start(bf16[2064,128]{1,0:T(8,128)(2,1)S(1)} %shard_map.46.refs_2_.refs_4_.refs_1_), channel_id=1, source_target_pairs={{0,1022},{1,1023},{2,0},{3,1},{4,2},{5,3},{6,4},{7,5},{8,6},{9,7},... | collective-permute-start | bytes 1585160 | tf_op jit(solution)/shard_map/ppermute | solution.py:211
  32.4 0.0 collective-permute-done.refs_1_.refs_0_
  32.5 1.9 %collective-permute-start.1 = (bf16[2064,128]{1,0:T(8,128)(2,1)S(1)}, bf16[2064,128]{1,0:T(8,128)(2,1)S(1)}, u32[]{:S(2)}, u32[]{:S(2)}) collective-permute-start(bf16[2064,128]{1,0:T(8,128)(2,1)S(1)} %slice.4.refs_3_.refs_5_.refs_1_), channel_id=1, source_target_pairs={{0,2},{1,3},{2,4},{3,5},{4,6},{5,7},{6,8},{7,9},{8,10},{9,11},{10,... | collective-permute-start | bytes 1585160 | tf_op jit(solution)/shard_map/ppermute | solution.py:211
  34.4 8.8 %collective-permute-start.2 = (bf16[2064,128]{1,0:T(8,128)(2,1)S(1)}, bf16[2064,128]{1,0:T(8,128)(2,1)S(1)}, u32[]{:S(2)}, u32[]{:S(2)}) collective-permute-start(bf16[2064,128]{1,0:T(8,128)(2,1)S(1)} %slice.4.refs_3_.refs_5_.refs_1_), channel_id=1, source_target_pairs={{0,1022},{1,1023},{2,0},{3,1},{4,2},{5,3},{6,4},{7,5},{8,6},{9,7},... | collective-permute-start | bytes 1585160 | tf_op jit(solution)/shard_map/ppermute | solution.py:211
  43.2 2.5 %shard_map.48 = (f32[1024,128]{1,0:T(8,128)S(1)}, f32[16,128]{1,0:T(8,128)S(1)}, f32[1024,128]{1,0:T(8,128)S(1)}, f32[16,128]{1,0:T(8,128)S(1)}) custom-call(bf16[1024,128]{1,0:T(8,128)(2,1)S(1)} %get-tuple-element.38.refs_0_, bf16[3088,128]{1,0:T(8,128)(2,1)S(1)} %collective-permute-done.refs_1_.refs_0_, ...), custom_call_target="tpu_custom_call" | custom-call | flops 268435456 | bytes 3145728 | tf_op jit(solution)/shard_map/pallas_call | solution.py:160
  45.7 0.0 collective-permute-done.3.refs_4_
  45.7 0.0 collective-permute-done.4.refs_5_
  45.7 1.9 %collective-permute-start.7 = (bf16[2064,128]{1,0:T(8,128)(2,1)S(1)}, bf16[2064,128]{1,0:T(8,128)(2,1)S(1)}, u32[]{:S(2)}, u32[]{:S(2)}) collective-permute-start(bf16[2064,128]{1,0:T(8,128)(2,1)S(1)} %collective-permute-done.3.refs_4_), channel_id=1, source_target_pairs={{0,2},{1,3},{2,4},{3,5},{4,6},{5,7},{6,8},{7,9},{8,10},{9,11},{10,... | collective-permute-start | bytes 1585160 | tf_op jit(solution)/shard_map/ppermute | solution.py:211
  47.6 8.8 %collective-permute-start.8 = (bf16[2064,128]{1,0:T(8,128)(2,1)S(1)}, bf16[2064,128]{1,0:T(8,128)(2,1)S(1)}, u32[]{:S(2)}, u32[]{:S(2)}) collective-permute-start(bf16[2064,128]{1,0:T(8,128)(2,1)S(1)} %collective-permute-done.4.refs_5_), channel_id=1, source_target_pairs={{0,1022},{1,1023},{2,0},{3,1},{4,2},{5,3},{6,4},{7,5},{8,6},{9,7},... | collective-permute-start | bytes 1585160 | tf_op jit(solution)/shard_map/ppermute | solution.py:211
  56.4 2.5 %shard_map.49 = (f32[1024,128]{1,0:T(8,128)S(1)}, f32[16,128]{1,0:T(8,128)S(1)}, f32[1024,128]{1,0:T(8,128)S(1)}, f32[16,128]{1,0:T(8,128)S(1)}) custom-call(bf16[1024,128]{1,0:T(8,128)(2,1)S(1)} %get-tuple-element.38.refs_0_, bf16[3088,128]{1,0:T(8,128)(2,1)S(1)} %collective-permute-done.refs_1_.refs_0_, ...), custom_call_target="tpu_custom_call" | custom-call | flops 268435456 | bytes 3145728 | tf_op jit(solution)/shard_map/pallas_call | solution.py:160
  58.9 0.0 collective-permute-done.1.refs_4_
  59.0 0.0 collective-permute-done.2.refs_5_
  59.0 1.9 %collective-permute-start.5 = (bf16[2064,128]{1,0:T(8,128)(2,1)S(1)}, bf16[2064,128]{1,0:T(8,128)(2,1)S(1)}, u32[]{:S(2)}, u32[]{:S(2)}) collective-permute-start(bf16[2064,128]{1,0:T(8,128)(2,1)S(1)} %collective-permute-done.1.refs_4_), channel_id=1, source_target_pairs={{0,2},{1,3},{2,4},{3,5},{4,6},{5,7},{6,8},{7,9},{8,10},{9,11},{10,... | collective-permute-start | bytes 1585160 | tf_op jit(solution)/shard_map/ppermute | solution.py:211
  60.9 8.8 %collective-permute-start.6 = (bf16[2064,128]{1,0:T(8,128)(2,1)S(1)}, bf16[2064,128]{1,0:T(8,128)(2,1)S(1)}, u32[]{:S(2)}, u32[]{:S(2)}) collective-permute-start(bf16[2064,128]{1,0:T(8,128)(2,1)S(1)} %collective-permute-done.2.refs_5_), channel_id=1, source_target_pairs={{0,1022},{1,1023},{2,0},{3,1},{4,2},{5,3},{6,4},{7,5},{8,6},{9,7},... | collective-permute-start | bytes 1585160 | tf_op jit(solution)/shard_map/ppermute | solution.py:211
  69.7 0.0 collective-permute-done.7.refs_6_
  69.7 0.0 collective-permute-done.8.refs_7_
  69.7 3.5 %shard_map.50 = (f32[1024,128]{1,0:T(8,128)S(1)}, f32[16,128]{1,0:T(8,128)S(1)}, f32[1024,128]{1,0:T(8,128)S(1)}, f32[16,128]{1,0:T(8,128)S(1)}) custom-call(bf16[1024,128]{1,0:T(8,128)(2,1)S(1)} %get-tuple-element.38.refs_0_, bf16[3088,128]{1,0:T(8,128)(2,1)S(1)} %collective-permute-done.refs_1_.refs_0_, ...), custom_call_target="tpu_custom_call" | custom-call | flops 536870912 | bytes 4194304 | tf_op jit(solution)/shard_map/pallas_call | solution.py:160
  73.2 5.3 %collective-permute-done.5.refs_2_ = bf16[2064,128]{1,0:T(8,128)(2,1)S(1)} collective-permute-done((bf16[2064,128]{1,0:T(8,128)(2,1)S(1)}, bf16[2064,128]{1,0:T(8,128)(2,1)S(1)}, u32[]{:S(2)}, u32[]{:S(2)}) %collective-permute-start.5) | collective-permute-done | bytes 528416 | tf_op jit(solution)/shard_map/ppermute | solution.py:211
  78.4 0.9 %collective-permute-done.6.refs_3_ = bf16[2064,128]{1,0:T(8,128)(2,1)S(1)} collective-permute-done((bf16[2064,128]{1,0:T(8,128)(2,1)S(1)}, bf16[2064,128]{1,0:T(8,128)(2,1)S(1)}, u32[]{:S(2)}, u32[]{:S(2)}) %collective-permute-start.6) | collective-permute-done | bytes 528416 | tf_op jit(solution)/shard_map/ppermute | solution.py:211
  79.3 0.9 %shard_map.52 = bf16[1024,128]{1,0:T(8,128)(2,1)S(1)} custom-call(bf16[3088,128]{1,0:T(8,128)(2,1)S(1)} %collective-permute-done.refs_1_.refs_0_, bf16[2064,128]{1,0:T(8,128)(2,1)S(1)} %slice.4.refs_3_.refs_5_.refs_1_, bf16[2064,128]{1,0:T(8,128)(2,1)S(1)} %collective-permute-done.5.refs_2_, bf16[2064,128]{1,0:T(8,128)(2,1)S(1)} %collective-permute-done.6.refs_3_, ...), custom_call_target="tpu_custom_call" | custom-call | flops 134217728 | bytes 2097152 | tf_op jit(solution)/shard_map/pallas_call | solution.py:160
  80.3 4.5 %collective-permute-start.9 = (bf16[1024,128]{1,0:T(8,128)(2,1)S(1)}, bf16[1024,128]{1,0:T(8,128)(2,1)S(1)}, u32[]{:S(2)}, u32[]{:S(2)}) collective-permute-start(bf16[1024,128]{1,0:T(8,128)(2,1)S(1)} %shard_map.52), channel_id=1, source_target_pairs={{0,1},{1,0},{2,3},{3,2},{4,5},{5,4},{6,7},{7,6},{8,9},{9,8},{10,11... | collective-permute-start | bytes 786440 | tf_op jit(solution)/shard_map/ppermute | solution.py:214
  84.8 0.9 %shard_map.51.o_mine = bf16[1024,128]{1,0:T(8,128)(2,1)S(1)} custom-call(bf16[1024,128]{1,0:T(8,128)(2,1)S(1)} %get-tuple-element.38.refs_0_, bf16[2064,128]{1,0:T(8,128)(2,1)S(1)} %shard_map.46.refs_2_.refs_4_.refs_1_, bf16[2064,128]{1,0:T(8,128)(2,1)S(1)} %collective-permute-done.5.refs_2_, bf16[2064,128]{1,0:T(8,128)(2,1)S(1)} %collective-permute-done.6.refs_3_, ...), custom_call_target="tpu_custom_call" | custom-call | flops 134217728 | bytes 2097152 | tf_op jit(solution)/shard_map/pallas_call | solution.py:160
  85.7 0.2 collective-permute-done.9.o_back
  85.9 0.9 %place.1 = bf16[128,2048]{1,0:T(8,128)(2,1)} custom-call(s32[1]{0:T(128)} %bitcast.core_ref, bf16[1024,128]{1,0:T(8,128)(2,1)S(1)} %shard_map.51.o_mine, bf16[1024,128]{1,0:T(8,128)(2,1)S(1)} %collective-permute-done.9.o_back), custom_call_target="tpu_custom_call" | custom-call | tf_op jit(solution)/shard_map/place/pallas_call | solution.py:194
  (1 shorter events, 0.0 us)
Async XLA Ops:
  0.0 0.7 copy-start.3
  0.7 1.0 %copy-start = (bf16[128,2048]{1,0:T(8,128)(2,1)S(1)}, bf16[128,2048]{1,0:T(8,128)(2,1)}, u32[]{:S(2)}) copy-start(bf16[128,2048]{1,0:T(8,128)(2,1)} %k_ref.2) | copy-start | bytes 1572868
  1.7 1.0 %copy-start.1 = (bf16[128,2048]{1,0:T(8,128)(2,1)S(1)}, bf16[128,2048]{1,0:T(8,128)(2,1)}, u32[]{:S(2)}) copy-start(bf16[128,2048]{1,0:T(8,128)(2,1)} %v_ref.2) | copy-start | bytes 1572868
  2.7 1.0 %copy-start.2 = (bf16[128,2048]{1,0:T(8,128)(2,1)S(1)}, bf16[128,2048]{1,0:T(8,128)(2,1)}, u32[]{:S(2)}) copy-start(bf16[128,2048]{1,0:T(8,128)(2,1)} %q_mine) | copy-start | bytes 1572868
  4.0 28.4 %collective-permute-start = (bf16[3088,128]{1,0:T(8,128)(2,1)S(1)}, bf16[3088,128]{1,0:T(8,128)(2,1)S(1)}, u32[]{:S(2)}, u32[]{:S(2)}) collective-permute-start(bf16[3088,128]{1,0:T(8,128)(2,1)S(1)} %get-tuple-element.40), channel_id=1, source_target_pairs={{0,1},{1,0},{2,3},{3,2},{4,5},{5,4},{6,7},{7,6},{8,9},{9,8},{10,11... | collective-permute-start | bytes 2371592 | tf_op jit(solution)/shard_map/ppermute | solution.py:214
  20.1 25.6 %collective-permute-start.3 = (bf16[2064,128]{1,0:T(8,128)(2,1)S(1)}, bf16[2064,128]{1,0:T(8,128)(2,1)S(1)}, u32[]{:S(2)}, u32[]{:S(2)}) collective-permute-start(bf16[2064,128]{1,0:T(8,128)(2,1)S(1)} %shard_map.46.refs_2_.refs_4_.refs_1_), channel_id=1, source_target_pairs={{0,2},{1,3},{2,4},{3,5},{4,6},{5,7},{6,8},{7,9},{8,10},{9,11},{10,... | collective-permute-start | bytes 1585160 | tf_op jit(solution)/shard_map/ppermute | solution.py:211
  22.0 23.7 %collective-permute-start.4 = (bf16[2064,128]{1,0:T(8,128)(2,1)S(1)}, bf16[2064,128]{1,0:T(8,128)(2,1)S(1)}, u32[]{:S(2)}, u32[]{:S(2)}) collective-permute-start(bf16[2064,128]{1,0:T(8,128)(2,1)S(1)} %shard_map.46.refs_2_.refs_4_.refs_1_), channel_id=1, source_target_pairs={{0,1022},{1,1023},{2,0},{3,1},{4,2},{5,3},{6,4},{7,5},{8,6},{9,7},... | collective-permute-start | bytes 1585160 | tf_op jit(solution)/shard_map/ppermute | solution.py:211
  32.5 26.5 %collective-permute-start.1 = (bf16[2064,128]{1,0:T(8,128)(2,1)S(1)}, bf16[2064,128]{1,0:T(8,128)(2,1)S(1)}, u32[]{:S(2)}, u32[]{:S(2)}) collective-permute-start(bf16[2064,128]{1,0:T(8,128)(2,1)S(1)} %slice.4.refs_3_.refs_5_.refs_1_), channel_id=1, source_target_pairs={{0,2},{1,3},{2,4},{3,5},{4,6},{5,7},{6,8},{7,9},{8,10},{9,11},{10,... | collective-permute-start | bytes 1585160 | tf_op jit(solution)/shard_map/ppermute | solution.py:211
  34.4 24.5 %collective-permute-start.2 = (bf16[2064,128]{1,0:T(8,128)(2,1)S(1)}, bf16[2064,128]{1,0:T(8,128)(2,1)S(1)}, u32[]{:S(2)}, u32[]{:S(2)}) collective-permute-start(bf16[2064,128]{1,0:T(8,128)(2,1)S(1)} %slice.4.refs_3_.refs_5_.refs_1_), channel_id=1, source_target_pairs={{0,1022},{1,1023},{2,0},{3,1},{4,2},{5,3},{6,4},{7,5},{8,6},{9,7},... | collective-permute-start | bytes 1585160 | tf_op jit(solution)/shard_map/ppermute | solution.py:211
  45.7 24.0 %collective-permute-start.7 = (bf16[2064,128]{1,0:T(8,128)(2,1)S(1)}, bf16[2064,128]{1,0:T(8,128)(2,1)S(1)}, u32[]{:S(2)}, u32[]{:S(2)}) collective-permute-start(bf16[2064,128]{1,0:T(8,128)(2,1)S(1)} %collective-permute-done.3.refs_4_), channel_id=1, source_target_pairs={{0,2},{1,3},{2,4},{3,5},{4,6},{5,7},{6,8},{7,9},{8,10},{9,11},{10,... | collective-permute-start | bytes 1585160 | tf_op jit(solution)/shard_map/ppermute | solution.py:211
  47.6 22.1 %collective-permute-start.8 = (bf16[2064,128]{1,0:T(8,128)(2,1)S(1)}, bf16[2064,128]{1,0:T(8,128)(2,1)S(1)}, u32[]{:S(2)}, u32[]{:S(2)}) collective-permute-start(bf16[2064,128]{1,0:T(8,128)(2,1)S(1)} %collective-permute-done.4.refs_5_), channel_id=1, source_target_pairs={{0,1022},{1,1023},{2,0},{3,1},{4,2},{5,3},{6,4},{7,5},{8,6},{9,7},... | collective-permute-start | bytes 1585160 | tf_op jit(solution)/shard_map/ppermute | solution.py:211
  59.0 19.5 %collective-permute-start.5 = (bf16[2064,128]{1,0:T(8,128)(2,1)S(1)}, bf16[2064,128]{1,0:T(8,128)(2,1)S(1)}, u32[]{:S(2)}, u32[]{:S(2)}) collective-permute-start(bf16[2064,128]{1,0:T(8,128)(2,1)S(1)} %collective-permute-done.1.refs_4_), channel_id=1, source_target_pairs={{0,2},{1,3},{2,4},{3,5},{4,6},{5,7},{6,8},{7,9},{8,10},{9,11},{10,... | collective-permute-start | bytes 1585160 | tf_op jit(solution)/shard_map/ppermute | solution.py:211
  60.9 18.5 %collective-permute-start.6 = (bf16[2064,128]{1,0:T(8,128)(2,1)S(1)}, bf16[2064,128]{1,0:T(8,128)(2,1)S(1)}, u32[]{:S(2)}, u32[]{:S(2)}) collective-permute-start(bf16[2064,128]{1,0:T(8,128)(2,1)S(1)} %collective-permute-done.2.refs_5_), channel_id=1, source_target_pairs={{0,1022},{1,1023},{2,0},{3,1},{4,2},{5,3},{6,4},{7,5},{8,6},{9,7},... | collective-permute-start | bytes 1585160 | tf_op jit(solution)/shard_map/ppermute | solution.py:211
  80.3 5.6 %collective-permute-start.9 = (bf16[1024,128]{1,0:T(8,128)(2,1)S(1)}, bf16[1024,128]{1,0:T(8,128)(2,1)S(1)}, u32[]{:S(2)}, u32[]{:S(2)}) collective-permute-start(bf16[1024,128]{1,0:T(8,128)(2,1)S(1)} %shard_map.52), channel_id=1, source_target_pairs={{0,1},{1,0},{2,3},{3,2},{4,5},{5,4},{6,7},{7,6},{8,9},{9,8},{10,11... | collective-permute-start | bytes 786440 | tf_op jit(solution)/shard_map/ppermute | solution.py:214
where the time goes:
time: 87.4 us; the launch traced here: 86.8 us
  starting transfers between devices  65 us (74%)
  Pallas kernels  11.7 us (13%)
  waiting for transfers between devices  6.38 us (7%)
  local copies, waits for them, and re-layouts  3.62 us (4%)
    ppermute x8, starting transfers between devices, shift(): lax.ppermute(x, AXES, [(d, (d + steps) % count) for d in range(count)])  44.5 us
    ppermute x2, starting transfers between devices, swap(): return lax.ppermute(x, AXES, [(d, d ^ 1) for d in range(count)])  20.5 us
    pallas_call x5, Pallas kernels, attend(): pl.pallas_call(functools.partial(attend_kernel, heads, tokens, groups, n_...  10.3 us
    ppermute x8, waiting for transfers between devices, shift(): lax.ppermute(x, AXES, [(d, (d + steps) % count) for d in range(count)])  6.18 us
    unnamed x8, local copies, waits for them, and re-layouts  3.59 us
  transfers between devices with their start and end apart: 10, of which 3 were waited for; matrix products, arithmetic and copies ran while one was open for 0% of the time, Pallas kernels for 11%

commit v1 on v0

--- a/solution.py
+++ b/solution.py
@@ -13,75 +13,92 @@
 AXES = ("blk", "head")
 NEG = -1e30
 VMEM_LIMIT = 16 << 20
+WHOLE_VMEM = 67043328
 F32 = jnp.float32
 BF16 = jnp.bfloat16
 
 
-def pack_half(k_ref, v_ref, ids_ref, out_ref):
-    tokens = k_ref.shape[0]
-    heads = k_ref.shape[1] // HD
+def load_halves(loads, sems):
+    copies = []
+    for n, (source, half_index, dest, at) in enumerate(loads):
+        tokens, width = source.shape
+        heads = width // 2 // HD
+        for head in range(heads):
+            first_col = pl.multiple_of(half_index * (width // 2) + head * HD, HD)
+            rows = slice(at + head * tokens, at + (head + 1) * tokens)
+            copy = pltpu.make_async_copy(source.at[:, pl.ds(first_col, HD)], dest.at[rows, :], sems.at[n, head])
+            copy.start()
+            copies.append(copy)
+    return copies
+
+
+def finish_pack(ids_ref, v_buf, out_ref, v_copies):
+    tokens = ids_ref.shape[1]
+    heads = v_buf.shape[0] // tokens
     full = heads * tokens
-    for head in range(heads):
-        cols = slice(head * HD, (head + 1) * HD)
-        rows = head * tokens
-        out_ref[rows : rows + tokens, :] = k_ref[:, cols]
-        out_ref[full + rows : full + rows + tokens, :] = v_ref[:, cols].T
     ids = ids_ref[...] + 1
     row = lax.broadcasted_iota(jnp.int32, (16, tokens), 0)
     tile = jnp.where(row == 0, ids >> 4, jnp.where(row == 1, ids & 15, 0)).astype(F32).astype(BF16)
     out_ref[2 * full : 2 * full + 16, :] = tile
-
-
-def pack_mine_kernel(core_ref, k_ref, v_ref, ids_ref, kv_out):
-    pack_half(k_ref, v_ref, ids_ref, kv_out)
-
-
-def pack_other_kernel(core_ref, k_ref, v_ref, q_other, q_mine, ids_ref, kvq_out, q_out):
-    pack_half(k_ref, v_ref, ids_ref, kvq_out)
-    tokens = k_ref.shape[0]
-    heads = k_ref.shape[1] // HD
+    for head in range(heads):
+        v_copies[head].wait()
+        rows = head * tokens
+        out_ref[full + rows : full + rows + tokens, :] = v_buf[rows : rows + tokens, :].T
+
+
+def pack_mine_kernel(core_ref, k_hbm, v_hbm, ids_hbm, out_ref, v_buf, ids_buf, sems, id_sem):
+    core = core_ref[0]
+    heads = k_hbm.shape[1] // 2 // HD
+    id_copy = pltpu.make_async_copy(ids_hbm, ids_buf, id_sem)
+    id_copy.start()
+    copies = load_halves([(v_hbm, core, v_buf, 0), (k_hbm, core, out_ref, 0)], sems)
+    id_copy.wait()
+    finish_pack(ids_buf, v_buf, out_ref, copies[:heads])
+    for copy in copies[heads:]:
+        copy.wait()
+
+
+def pack_other_kernel(core_ref, k_hbm, v_hbm, q_hbm, ids_hbm, out_ref, q_out, v_buf, ids_buf, sems, id_sem):
+    core = core_ref[0]
+    tokens = k_hbm.shape[0]
+    heads = k_hbm.shape[1] // 2 // HD
     at = 2 * heads * tokens + 16
-    for head in range(heads):
-        cols = slice(head * HD, (head + 1) * HD)
-        rows = head * tokens
-        kvq_out[at + rows : at + rows + tokens, :] = q_other[:, cols]
-        q_out[rows : rows + tokens, :] = q_mine[:, cols]
+    id_copy = pltpu.make_async_copy(ids_hbm, ids_buf, id_sem)
+    id_copy.start()
+    copies = load_halves(
+        [(v_hbm, 1 - core, v_buf, 0), (k_hbm, 1 - core, out_ref, 0), (q_hbm, 1 - core, out_ref, at), (q_hbm, core, q_out, 0)], sems
+    )
+    id_copy.wait()
+    finish_pack(ids_buf, v_buf, out_ref, copies[:heads])
+    for copy in copies[heads:]:
+        copy.wait()
 
 
 def pack(core, queries, keys, values, ids):
     tokens, width = queries.shape
-    half = width // 2
-    heads = half // HD
-    mine = pl.BlockSpec((tokens, half), lambda i, c: (0, c[0]))
-    other = pl.BlockSpec((tokens, half), lambda i, c: (0, 1 - c[0]))
-    id_spec = pl.BlockSpec((1, tokens), lambda i, c: (0, 0))
+    heads = width // 2 // HD
     rows = heads * tokens
-
-    def whole(n):
-        return pl.BlockSpec((n, HD), lambda i, c: (0, 0))
-
-    def call(kernel, in_specs, sizes, *args):
+    hbm = pl.BlockSpec(memory_space=pltpu.HBM)
+    vmem = pl.BlockSpec(memory_space=pltpu.VMEM)
+
+    def call(kernel, n_loads, sizes, limit, *args):
         return pl.pallas_call(
             kernel,
-            grid_spec=pltpu.PrefetchScalarGridSpec(
-                num_scalar_prefetch=1, grid=(1,), in_specs=in_specs, out_specs=[whole(n) for n in sizes]
-            ),
+            in_specs=[pl.BlockSpec(memory_space=pltpu.SMEM)] + [hbm] * len(args),
+            out_specs=[vmem for n in sizes],
             out_shape=[jax.ShapeDtypeStruct((n, HD), BF16) for n in sizes],
-            compiler_params=pltpu.CompilerParams(vmem_limit_bytes=VMEM_LIMIT),
+            scratch_shapes=[
+                pltpu.VMEM((rows, HD), BF16),
+                pltpu.VMEM((1, tokens), jnp.int32),
+                pltpu.SemaphoreType.DMA((n_loads, heads)),
+                pltpu.SemaphoreType.DMA(()),
+            ],
+            compiler_params=pltpu.CompilerParams(vmem_limit_bytes=limit),
         )(core, *args)
 
-    (kv,) = call(pack_mine_kernel, [mine, mine, id_spec], [2 * rows + 16], keys, values, ids)
+    (kv,) = call(pack_mine_kernel, 2, [2 * rows + 16], WHOLE_VMEM, keys, values, ids)
     keys, values, queries, kv = lax.optimization_barrier((keys, values, queries, kv))
-    kvq, q = call(
-        pack_other_kernel,
-        [other, other, other, mine, id_spec],
-        [3 * rows + 16, rows],
-        keys,
-        values,
-        queries,
-        queries,
-        ids,
-    )
+    kvq, q = call(pack_other_kernel, 4, [3 * rows + 16, rows], WHOLE_VMEM, keys, values, queries, ids)
     return kv, kvq, q
 
 
@@ -207,33 +224,39 @@
     core = lax.axis_index("head") % 2
     core_arr = core.reshape(1).astype(jnp.int32)
 
-    def shift(x, steps):
-        return lax.ppermute(x, AXES, [(d, (d + steps) % count) for d in range(count)])
+    chips = count // 2
 
     def swap(x):
         return lax.ppermute(x, AXES, [(d, d ^ 1) for d in range(count)])
 
+    def pair_a(x):
+        return lax.ppermute(x, AXES, [(d, d ^ 2) for d in range(count)])
+
+    def pair_b(x):
+        ups = [(2 * c + i, 2 * c + 2 + i) for c in range(1, chips - 1, 2) for i in range(2)]
+        return lax.ppermute(x, AXES, ups + [(v, u) for u, v in ups])
+
     kv, kvq, q = pack(core_arr, queries, key_feats, value_feats, segment_ids.reshape(1, tokens))
-    up1 = shift(kv, 2)
-    down1 = shift(kv, -2)
+    a1 = pair_a(kv)
+    b1 = pair_b(kv)
     kvq2 = swap(kvq)
     kv2 = kvq2[: kv.shape[0]]
-    up1b = shift(kv2, 2)
-    down1b = shift(kv2, -2)
+    a1b = pair_a(kv2)
+    b1b = pair_b(kv2)
     heads = width // 2 // HD
     qs, qids = [q, kvq2], [kv, kv2]
     carry = attend(heads, qs, qids, [kv, kv2], [], False)
-    up1, down1, carry = lax.optimization_barrier((up1, down1, carry))
-    up2 = shift(up1, 2)
-    down2 = shift(down1, -2)
-    carry = attend(heads, qs, qids, [up1, down1], carry, False)
-    up1b, down1b, carry = lax.optimization_barrier((up1b, down1b, carry))
-    up2b = shift(up1b, 2)
-    down2b = shift(down1b, -2)
-    carry = attend(heads, qs, qids, [up1b, down1b, up2, down2], carry, False)
-    (o_other,) = attend(heads, [kvq2], [kv2], [up2b, down2b], [carry[1]], True)
+    a1, b1, carry = lax.optimization_barrier((a1, b1, carry))
+    a2 = pair_a(b1)
+    b2 = pair_b(a1)
+    carry = attend(heads, qs, qids, [a1, b1], carry, False)
+    a1b, b1b, carry = lax.optimization_barrier((a1b, b1b, carry))
+    a2b = pair_a(b1b)
+    b2b = pair_b(a1b)
+    carry = attend(heads, qs, qids, [a1b, b1b, a2, b2], carry, False)
+    (o_other,) = attend(heads, [kvq2], [kv2], [a2b, b2b], [carry[1]], True)
     back = swap(o_other)
-    (o_mine,) = attend(heads, [q], [kv], [up2b, down2b], [carry[0]], True)
+    (o_mine,) = attend(heads, [q], [kv], [a2b, b2b], [carry[0]], True)
     return place(core_arr, o_mine, back, tokens, width)
 
 

time: 87.4 us -> 85.5 us (0.978)
  the two profiles are of different devices: /device:TPU:1 before, /device:TPU:8 now
where the time goes in v1:
time: 85.5 us; the launch traced here: 84.7 us
  starting transfers between devices  52.3 us (61%)
  Pallas kernels  16.7 us (20%)
  waiting for transfers between devices  15.5 us (18%)
    ppermute x4, starting transfers between devices, pair_b(): return lax.ppermute(x, AXES, ups + [(v, u) for u, v in ups])  37.4 us
    ppermute x4, waiting for transfers between devices, pair_b(): return lax.ppermute(x, AXES, ups + [(v, u) for u, v in ups])  12.7 us
    ppermute x4, starting transfers between devices, pair_a(): return lax.ppermute(x, AXES, [(d, d ^ 2) for d in range(count)])  10.9 us
    pallas_call x5, Pallas kernels, attend(): pl.pallas_call(functools.partial(attend_kernel, heads, tokens, groups, n_...  10.3 us
    pallas_call x2, Pallas kernels, call(): pl.pallas_call(kernel, in_specs=[pl.BlockSpec(memory_space=pltpu.SMEM)] +...  5.46 us
    ppermute x2, starting transfers between devices, swap(): return lax.ppermute(x, AXES, [(d, d ^ 1) for d in range(count)])  3.97 us
    ppermute x4, waiting for transfers between devices, pair_a(): return lax.ppermute(x, AXES, [(d, d ^ 2) for d in range(count)])  2.16 us
  transfers between devices with their start and end apart: 10, of which 5 were waited for; matrix products, arithmetic and copies ran while one was open for 0% of the time, Pallas kernels for 11%

profile of v1, /device:TPU:8, one launch (start us, length us, event | category | flops | bytes accessed | tf_op | source)
XLA Modules:
  0.0 84.7 jit_solution(6328745054102112324)
XLA Ops:
  0.0 2.5 %shard_map.46.refs_2_.refs_4_.refs_1_ = bf16[2064,128]{1,0:T(8,128)(2,1)} custom-call(s32[1]{0:T(128)} %bitcast.core_ref, bf16[128,2048]{1,0:T(8,128)(2,1)} %k_hbm.2, bf16[128,2048]{1,0:T(8,128)(2,1)} %v_hbm.2, s32[1,128]{1,0:T(1,128)} %bitcast.2), custom_call_target="tpu_custom_call" | custom-call | tf_op jit(solution)/shard_map/pallas_call | solution.py:85
  2.5 3.0 %shard_map.47 = (bf16[3088,128]{1,0:T(8,128)(2,1)}, bf16[1024,128]{1,0:T(8,128)(2,1)}) custom-call(s32[1]{0:T(128)} %bitcast.core_ref, bf16[128,2048]{1,0:T(8,128)(2,1)} %k_hbm.2, bf16[128,2048]{1,0:T(8,128)(2,1)} %v_hbm.2, bf16[128,2048]{1,0:T(8,128)(2,1)} %q_hbm, s32[1,128]{1,0:T(1,128)} %bitcast.3), custom_call_target="tpu_custom_call" | custom-call | tf_op jit(solution)/shard_map/pallas_call | solution.py:85
  5.5 0.0 copy-start
  5.5 0.0 copy-start.1
  5.5 2.1 %collective-permute-start = (bf16[3088,128]{1,0:T(8,128)(2,1)}, bf16[3088,128]{1,0:T(8,128)(2,1)S(1)}, u32[]{:S(2)}, u32[]{:S(2)}) collective-permute-start(bf16[3088,128]{1,0:T(8,128)(2,1)} %get-tuple-element.40), channel_id=1, source_target_pairs={{0,1},{1,0},{2,3},{3,2},{4,5},{5,4},{6,7},{7,6},{8,9},{9,8},{10,11... | collective-permute-start | bytes 2371592 | tf_op jit(solution)/shard_map/ppermute | solution.py:230
  7.6 5.2 %collective-permute-start.3 = (bf16[2064,128]{1,0:T(8,128)(2,1)}, bf16[2064,128]{1,0:T(8,128)(2,1)S(1)}, u32[]{:S(2)}, u32[]{:S(2)}) collective-permute-start(bf16[2064,128]{1,0:T(8,128)(2,1)} %shard_map.46.refs_2_.refs_4_.refs_1_), channel_id=1, source_target_pairs={{0,2},{1,3},{2,0},{3,1},{4,6},{5,7},{6,4},{7,5},{8,10},{9,11},{10,... | collective-permute-start | bytes 1585160 | tf_op jit(solution)/shard_map/ppermute | solution.py:233
  12.8 17.7 %collective-permute-start.4 = (bf16[2064,128]{1,0:T(8,128)(2,1)}, bf16[2064,128]{1,0:T(8,128)(2,1)S(1)}, u32[]{:S(2)}, u32[]{:S(2)}) collective-permute-start(bf16[2064,128]{1,0:T(8,128)(2,1)} %shard_map.46.refs_2_.refs_4_.refs_1_), channel_id=1, source_target_pairs={{2,4},{3,5},{6,8},{7,9},{10,12},{11,13},{14,16},{15,17},{18,20},{1... | collective-permute-start | bytes 1585160 | tf_op jit(solution)/shard_map/ppermute | solution.py:237
  30.5 0.0 collective-permute-done.refs_1_.refs_0_
  30.5 1.9 %collective-permute-start.1 = (bf16[2064,128]{1,0:T(8,128)(2,1)S(1)}, bf16[2064,128]{1,0:T(8,128)(2,1)S(1)}, u32[]{:S(2)}, u32[]{:S(2)}) collective-permute-start(bf16[2064,128]{1,0:T(8,128)(2,1)S(1)} %slice.4.refs_3_.refs_5_.refs_1_), channel_id=1, source_target_pairs={{0,2},{1,3},{2,0},{3,1},{4,6},{5,7},{6,4},{7,5},{8,10},{9,11},{10,... | collective-permute-start | bytes 1585160 | tf_op jit(solution)/shard_map/ppermute | solution.py:233
  32.5 3.9 %collective-permute-start.2 = (bf16[2064,128]{1,0:T(8,128)(2,1)S(1)}, bf16[2064,128]{1,0:T(8,128)(2,1)S(1)}, u32[]{:S(2)}, u32[]{:S(2)}) collective-permute-start(bf16[2064,128]{1,0:T(8,128)(2,1)S(1)} %slice.4.refs_3_.refs_5_.refs_1_), channel_id=1, source_target_pairs={{2,4},{3,5},{6,8},{7,9},{10,12},{11,13},{14,16},{15,17},{18,20},{1... | collective-permute-start | bytes 1585160 | tf_op jit(solution)/shard_map/ppermute | solution.py:237
  36.4 0.0 copy-done
  36.4 0.0 copy-done.1
  36.4 2.5 %shard_map.48 = (f32[1024,128]{1,0:T(8,128)S(1)}, f32[16,128]{1,0:T(8,128)S(1)}, f32[1024,128]{1,0:T(8,128)S(1)}, f32[16,128]{1,0:T(8,128)S(1)}) custom-call(bf16[1024,128]{1,0:T(8,128)(2,1)S(1)} %copy-done.1, bf16[3088,128]{1,0:T(8,128)(2,1)S(1)} %collective-permute-done.refs_1_.refs_0_, bf16[2064,128]{1,0:T(8,128)(2,1)S(1)} %copy-done, ...), custom_call_target="tpu_custom_call" | custom-call | flops 268435456 | bytes 3145728 | tf_op jit(solution)/shard_map/pallas_call | solution.py:177
  38.9 0.0 collective-permute-done.3.refs_4_
  38.9 4.6 %collective-permute-done.4.refs_5_ = bf16[2064,128]{1,0:T(8,128)(2,1)S(1)} collective-permute-done((bf16[2064,128]{1,0:T(8,128)(2,1)}, bf16[2064,128]{1,0:T(8,128)(2,1)S(1)}, u32[]{:S(2)}, u32[]{:S(2)}) %collective-permute-start.4) | collective-permute-done | bytes 528416 | tf_op jit(solution)/shard_map/ppermute | solution.py:237
  43.5 1.9 %collective-permute-start.7 = (bf16[2064,128]{1,0:T(8,128)(2,1)S(1)}, bf16[2064,128]{1,0:T(8,128)(2,1)S(1)}, u32[]{:S(2)}, u32[]{:S(2)}) collective-permute-start(bf16[2064,128]{1,0:T(8,128)(2,1)S(1)} %collective-permute-done.4.refs_5_), channel_id=1, source_target_pairs={{0,2},{1,3},{2,0},{3,1},{4,6},{5,7},{6,4},{7,5},{8,10},{9,11},{10,... | collective-permute-start | bytes 1585160 | tf_op jit(solution)/shard_map/ppermute | solution.py:233
  45.5 9.4 %collective-permute-start.8 = (bf16[2064,128]{1,0:T(8,128)(2,1)S(1)}, bf16[2064,128]{1,0:T(8,128)(2,1)S(1)}, u32[]{:S(2)}, u32[]{:S(2)}) collective-permute-start(bf16[2064,128]{1,0:T(8,128)(2,1)S(1)} %collective-permute-done.3.refs_4_), channel_id=1, source_target_pairs={{2,4},{3,5},{6,8},{7,9},{10,12},{11,13},{14,16},{15,17},{18,20},{1... | collective-permute-start | bytes 1585160 | tf_op jit(solution)/shard_map/ppermute | solution.py:237
  54.8 2.5 %shard_map.49 = (f32[1024,128]{1,0:T(8,128)S(1)}, f32[16,128]{1,0:T(8,128)S(1)}, f32[1024,128]{1,0:T(8,128)S(1)}, f32[16,128]{1,0:T(8,128)S(1)}) custom-call(bf16[1024,128]{1,0:T(8,128)(2,1)S(1)} %copy-done.1, bf16[3088,128]{1,0:T(8,128)(2,1)S(1)} %collective-permute-done.refs_1_.refs_0_, bf16[2064,128]{1,0:T(8,128)(2,1)S(1)} %copy-done, ...), custom_call_target="tpu_custom_call" | custom-call | flops 268435456 | bytes 3145728 | tf_op jit(solution)/shard_map/pallas_call | solution.py:177
  57.3 0.0 collective-permute-done.1.refs_4_
  57.3 0.0 collective-permute-done.2.refs_5_
  57.3 1.9 %collective-permute-start.5 = (bf16[2064,128]{1,0:T(8,128)(2,1)S(1)}, bf16[2064,128]{1,0:T(8,128)(2,1)S(1)}, u32[]{:S(2)}, u32[]{:S(2)}) collective-permute-start(bf16[2064,128]{1,0:T(8,128)(2,1)S(1)} %collective-permute-done.2.refs_5_), channel_id=1, source_target_pairs={{0,2},{1,3},{2,0},{3,1},{4,6},{5,7},{6,4},{7,5},{8,10},{9,11},{10,... | collective-permute-start | bytes 1585160 | tf_op jit(solution)/shard_map/ppermute | solution.py:233
  59.3 6.4 %collective-permute-start.6 = (bf16[2064,128]{1,0:T(8,128)(2,1)S(1)}, bf16[2064,128]{1,0:T(8,128)(2,1)S(1)}, u32[]{:S(2)}, u32[]{:S(2)}) collective-permute-start(bf16[2064,128]{1,0:T(8,128)(2,1)S(1)} %collective-permute-done.1.refs_4_), channel_id=1, source_target_pairs={{2,4},{3,5},{6,8},{7,9},{10,12},{11,13},{14,16},{15,17},{18,20},{1... | collective-permute-start | bytes 1585160 | tf_op jit(solution)/shard_map/ppermute | solution.py:237
  65.7 0.0 collective-permute-done.7.refs_6_
  65.7 0.7 collective-permute-done.8.refs_7_
  66.4 3.5 %shard_map.50 = (f32[1024,128]{1,0:T(8,128)S(1)}, f32[16,128]{1,0:T(8,128)S(1)}, f32[1024,128]{1,0:T(8,128)S(1)}, f32[16,128]{1,0:T(8,128)S(1)}) custom-call(bf16[1024,128]{1,0:T(8,128)(2,1)S(1)} %copy-done.1, bf16[3088,128]{1,0:T(8,128)(2,1)S(1)} %collective-permute-done.refs_1_.refs_0_, bf16[2064,128]{1,0:T(8,128)(2,1)S(1)} %copy-done, ...), custom_call_target="tpu_custom_call" | custom-call | flops 536870912 | bytes 4194304 | tf_op jit(solution)/shard_map/pallas_call | solution.py:177
  69.9 2.2 %collective-permute-done.5.refs_2_ = bf16[2064,128]{1,0:T(8,128)(2,1)S(1)} collective-permute-done((bf16[2064,128]{1,0:T(8,128)(2,1)S(1)}, bf16[2064,128]{1,0:T(8,128)(2,1)S(1)}, u32[]{:S(2)}, u32[]{:S(2)}) %collective-permute-start.5) | collective-permute-done | bytes 528416 | tf_op jit(solution)/shard_map/ppermute | solution.py:233
  72.0 7.4 %collective-permute-done.6.refs_3_ = bf16[2064,128]{1,0:T(8,128)(2,1)S(1)} collective-permute-done((bf16[2064,128]{1,0:T(8,128)(2,1)S(1)}, bf16[2064,128]{1,0:T(8,128)(2,1)S(1)}, u32[]{:S(2)}, u32[]{:S(2)}) %collective-permute-start.6) | collective-permute-done | bytes 528416 | tf_op jit(solution)/shard_map/ppermute | solution.py:237
  79.4 0.9 %shard_map.52 = bf16[1024,128]{1,0:T(8,128)(2,1)S(1)} custom-call(bf16[3088,128]{1,0:T(8,128)(2,1)S(1)} %collective-permute-done.refs_1_.refs_0_, bf16[2064,128]{1,0:T(8,128)(2,1)S(1)} %slice.4.refs_3_.refs_5_.refs_1_, bf16[2064,128]{1,0:T(8,128)(2,1)S(1)} %collective-permute-done.5.refs_2_, bf16[2064,128]{1,0:T(8,128)(2,1)S(1)} %collective-permute-done.6.refs_3_, ...), custom_call_target="tpu_custom_call" | custom-call | flops 134217728 | bytes 2097152 | tf_op jit(solution)/shard_map/pallas_call | solution.py:177
  80.3 1.9 %collective-permute-start.9 = (bf16[1024,128]{1,0:T(8,128)(2,1)S(1)}, bf16[1024,128]{1,0:T(8,128)(2,1)S(1)}, u32[]{:S(2)}, u32[]{:S(2)}) collective-permute-start(bf16[1024,128]{1,0:T(8,128)(2,1)S(1)} %shard_map.52), channel_id=1, source_target_pairs={{0,1},{1,0},{2,3},{3,2},{4,5},{5,4},{6,7},{7,6},{8,9},{9,8},{10,11... | collective-permute-start | bytes 786440 | tf_op jit(solution)/shard_map/ppermute | solution.py:230
  82.3 0.9 %shard_map.51.o_mine = bf16[1024,128]{1,0:T(8,128)(2,1)S(1)} custom-call(bf16[1024,128]{1,0:T(8,128)(2,1)S(1)} %copy-done.1, bf16[2064,128]{1,0:T(8,128)(2,1)S(1)} %copy-done, bf16[2064,128]{1,0:T(8,128)(2,1)S(1)} %collective-permute-done.5.refs_2_, bf16[2064,128]{1,0:T(8,128)(2,1)S(1)} %collective-permute-done.6.refs_3_, ...), custom_call_target="tpu_custom_call" | custom-call | flops 134217728 | bytes 2097152 | tf_op jit(solution)/shard_map/pallas_call | solution.py:177
  83.2 0.6 collective-permute-done.9.o_back
  83.8 0.9 %place.1 = bf16[128,2048]{1,0:T(8,128)(2,1)} custom-call(s32[1]{0:T(128)} %bitcast.core_ref, bf16[1024,128]{1,0:T(8,128)(2,1)S(1)} %shard_map.51.o_mine, bf16[1024,128]{1,0:T(8,128)(2,1)S(1)} %collective-permute-done.9.o_back), custom_call_target="tpu_custom_call" | custom-call | tf_op jit(solution)/shard_map/place/pallas_call | solution.py:211
  (1 shorter events, 0.0 us)
Async XLA Ops:
  5.5 30.9 %copy-start = (bf16[2064,128]{1,0:T(8,128)(2,1)S(1)}, bf16[2064,128]{1,0:T(8,128)(2,1)}, u32[]{:S(2)}) copy-start(bf16[2064,128]{1,0:T(8,128)(2,1)} %shard_map.46.refs_2_.refs_4_.refs_1_) | copy-start | bytes 1585156
  5.5 30.9 %copy-start.1 = (bf16[1024,128]{1,0:T(8,128)(2,1)S(1)}, bf16[1024,128]{1,0:T(8,128)(2,1)}, u32[]{:S(2)}) copy-start(bf16[1024,128]{1,0:T(8,128)(2,1)} %get-tuple-element.38.refs_0_) | copy-start | bytes 786436
  5.5 25.0 %collective-permute-start = (bf16[3088,128]{1,0:T(8,128)(2,1)}, bf16[3088,128]{1,0:T(8,128)(2,1)S(1)}, u32[]{:S(2)}, u32[]{:S(2)}) collective-permute-start(bf16[3088,128]{1,0:T(8,128)(2,1)} %get-tuple-element.40), channel_id=1, source_target_pairs={{0,1},{1,0},{2,3},{3,2},{4,5},{5,4},{6,7},{7,6},{8,9},{9,8},{10,11... | collective-permute-start | bytes 2371592 | tf_op jit(solution)/shard_map/ppermute | solution.py:230
  7.6 31.3 %collective-permute-start.3 = (bf16[2064,128]{1,0:T(8,128)(2,1)}, bf16[2064,128]{1,0:T(8,128)(2,1)S(1)}, u32[]{:S(2)}, u32[]{:S(2)}) collective-permute-start(bf16[2064,128]{1,0:T(8,128)(2,1)} %shard_map.46.refs_2_.refs_4_.refs_1_), channel_id=1, source_target_pairs={{0,2},{1,3},{2,0},{3,1},{4,6},{5,7},{6,4},{7,5},{8,10},{9,11},{10,... | collective-permute-start | bytes 1585160 | tf_op jit(solution)/shard_map/ppermute | solution.py:233
  12.8 30.8 %collective-permute-start.4 = (bf16[2064,128]{1,0:T(8,128)(2,1)}, bf16[2064,128]{1,0:T(8,128)(2,1)S(1)}, u32[]{:S(2)}, u32[]{:S(2)}) collective-permute-start(bf16[2064,128]{1,0:T(8,128)(2,1)} %shard_map.46.refs_2_.refs_4_.refs_1_), channel_id=1, source_target_pairs={{2,4},{3,5},{6,8},{7,9},{10,12},{11,13},{14,16},{15,17},{18,20},{1... | collective-permute-start | bytes 1585160 | tf_op jit(solution)/shard_map/ppermute | solution.py:237
  30.5 26.8 %collective-permute-start.1 = (bf16[2064,128]{1,0:T(8,128)(2,1)S(1)}, bf16[2064,128]{1,0:T(8,128)(2,1)S(1)}, u32[]{:S(2)}, u32[]{:S(2)}) collective-permute-start(bf16[2064,128]{1,0:T(8,128)(2,1)S(1)} %slice.4.refs_3_.refs_5_.refs_1_), channel_id=1, source_target_pairs={{0,2},{1,3},{2,0},{3,1},{4,6},{5,7},{6,4},{7,5},{8,10},{9,11},{10,... | collective-permute-start | bytes 1585160 | tf_op jit(solution)/shard_map/ppermute | solution.py:233
  32.5 24.9 %collective-permute-start.2 = (bf16[2064,128]{1,0:T(8,128)(2,1)S(1)}, bf16[2064,128]{1,0:T(8,128)(2,1)S(1)}, u32[]{:S(2)}, u32[]{:S(2)}) collective-permute-start(bf16[2064,128]{1,0:T(8,128)(2,1)S(1)} %slice.4.refs_3_.refs_5_.refs_1_), channel_id=1, source_target_pairs={{2,4},{3,5},{6,8},{7,9},{10,12},{11,13},{14,16},{15,17},{18,20},{1... | collective-permute-start | bytes 1585160 | tf_op jit(solution)/shard_map/ppermute | solution.py:237
  43.5 22.1 %collective-permute-start.7 = (bf16[2064,128]{1,0:T(8,128)(2,1)S(1)}, bf16[2064,128]{1,0:T(8,128)(2,1)S(1)}, u32[]{:S(2)}, u32[]{:S(2)}) collective-permute-start(bf16[2064,128]{1,0:T(8,128)(2,1)S(1)} %collective-permute-done.4.refs_5_), channel_id=1, source_target_pairs={{0,2},{1,3},{2,0},{3,1},{4,6},{5,7},{6,4},{7,5},{8,10},{9,11},{10,... | collective-permute-start | bytes 1585160 | tf_op jit(solution)/shard_map/ppermute | solution.py:233
  45.5 21.0 %collective-permute-start.8 = (bf16[2064,128]{1,0:T(8,128)(2,1)S(1)}, bf16[2064,128]{1,0:T(8,128)(2,1)S(1)}, u32[]{:S(2)}, u32[]{:S(2)}) collective-permute-start(bf16[2064,128]{1,0:T(8,128)(2,1)S(1)} %collective-permute-done.3.refs_4_), channel_id=1, source_target_pairs={{2,4},{3,5},{6,8},{7,9},{10,12},{11,13},{14,16},{15,17},{18,20},{1... | collective-permute-start | bytes 1585160 | tf_op jit(solution)/shard_map/ppermute | solution.py:237
  57.3 14.7 %collective-permute-start.5 = (bf16[2064,128]{1,0:T(8,128)(2,1)S(1)}, bf16[2064,128]{1,0:T(8,128)(2,1)S(1)}, u32[]{:S(2)}, u32[]{:S(2)}) collective-permute-start(bf16[2064,128]{1,0:T(8,128)(2,1)S(1)} %collective-permute-done.2.refs_5_), channel_id=1, source_target_pairs={{0,2},{1,3},{2,0},{3,1},{4,6},{5,7},{6,4},{7,5},{8,10},{9,11},{10,... | collective-permute-start | bytes 1585160 | tf_op jit(solution)/shard_map/ppermute | solution.py:233
  59.3 20.1 %collective-permute-start.6 = (bf16[2064,128]{1,0:T(8,128)(2,1)S(1)}, bf16[2064,128]{1,0:T(8,128)(2,1)S(1)}, u32[]{:S(2)}, u32[]{:S(2)}) collective-permute-start(bf16[2064,128]{1,0:T(8,128)(2,1)S(1)} %collective-permute-done.1.refs_4_), channel_id=1, source_target_pairs={{2,4},{3,5},{6,8},{7,9},{10,12},{11,13},{14,16},{15,17},{18,20},{1... | collective-permute-start | bytes 1585160 | tf_op jit(solution)/shard_map/ppermute | solution.py:237
  80.3 3.4 %collective-permute-start.9 = (bf16[1024,128]{1,0:T(8,128)(2,1)S(1)}, bf16[1024,128]{1,0:T(8,128)(2,1)S(1)}, u32[]{:S(2)}, u32[]{:S(2)}) collective-permute-start(bf16[1024,128]{1,0:T(8,128)(2,1)S(1)} %shard_map.52), channel_id=1, source_target_pairs={{0,1},{1,0},{2,3},{3,2},{4,5},{5,4},{6,7},{7,6},{8,9},{9,8},{10,11... | collective-permute-start | bytes 786440 | tf_op jit(solution)/shard_map/ppermute | solution.py:230

commit v2 on v1

--- a/solution.py
+++ b/solution.py
@@ -32,18 +32,21 @@
     return copies
 
 
-def finish_pack(ids_ref, v_buf, out_ref, v_copies):
+def finish_pack(ids_ref, v_buf, out_refs, v_copies):
     tokens = ids_ref.shape[1]
     heads = v_buf.shape[0] // tokens
     full = heads * tokens
     ids = ids_ref[...] + 1
     row = lax.broadcasted_iota(jnp.int32, (16, tokens), 0)
     tile = jnp.where(row == 0, ids >> 4, jnp.where(row == 1, ids & 15, 0)).astype(F32).astype(BF16)
-    out_ref[2 * full : 2 * full + 16, :] = tile
+    for out_ref in out_refs:
+        out_ref[2 * full : 2 * full + 16, :] = tile
     for head in range(heads):
         v_copies[head].wait()
         rows = head * tokens
-        out_ref[full + rows : full + rows + tokens, :] = v_buf[rows : rows + tokens, :].T
+        turned = v_buf[rows : rows + tokens, :].T
+        for out_ref in out_refs:
+            out_ref[full + rows : full + rows + tokens, :] = turned
 
 
 def pack_mine_kernel(core_ref, k_hbm, v_hbm, ids_hbm, out_ref, v_buf, ids_buf, sems, id_sem):
@@ -53,23 +56,28 @@
     id_copy.start()
     copies = load_halves([(v_hbm, core, v_buf, 0), (k_hbm, core, out_ref, 0)], sems)
     id_copy.wait()
-    finish_pack(ids_buf, v_buf, out_ref, copies[:heads])
+    finish_pack(ids_buf, v_buf, [out_ref], copies[:heads])
     for copy in copies[heads:]:
         copy.wait()
 
 
-def pack_other_kernel(core_ref, k_hbm, v_hbm, q_hbm, ids_hbm, out_ref, q_out, v_buf, ids_buf, sems, id_sem):
+def pack_other_kernel(core_ref, k_hbm, v_hbm, q_hbm, ids_hbm, kv_ref, kvq_ref, q_out, v_buf, ids_buf, sems, id_sem):
     core = core_ref[0]
     tokens = k_hbm.shape[0]
     heads = k_hbm.shape[1] // 2 // HD
     at = 2 * heads * tokens + 16
     id_copy = pltpu.make_async_copy(ids_hbm, ids_buf, id_sem)
     id_copy.start()
-    copies = load_halves(
-        [(v_hbm, 1 - core, v_buf, 0), (k_hbm, 1 - core, out_ref, 0), (q_hbm, 1 - core, out_ref, at), (q_hbm, core, q_out, 0)], sems
-    )
+    loads = [
+        (v_hbm, 1 - core, v_buf, 0),
+        (k_hbm, 1 - core, kv_ref, 0),
+        (k_hbm, 1 - core, kvq_ref, 0),
+        (q_hbm, 1 - core, kvq_ref, at),
+        (q_hbm, core, q_out, 0),
+    ]
+    copies = load_halves(loads, sems)
     id_copy.wait()
-    finish_pack(ids_buf, v_buf, out_ref, copies[:heads])
+    finish_pack(ids_buf, v_buf, [kv_ref, kvq_ref], copies[:heads])
     for copy in copies[heads:]:
         copy.wait()
 
@@ -98,8 +106,8 @@
 
     (kv,) = call(pack_mine_kernel, 2, [2 * rows + 16], WHOLE_VMEM, keys, values, ids)
     keys, values, queries, kv = lax.optimization_barrier((keys, values, queries, kv))
-    kvq, q = call(pack_other_kernel, 4, [3 * rows + 16, rows], WHOLE_VMEM, keys, values, queries, ids)
-    return kv, kvq, q
+    kvo, kvq, q = call(pack_other_kernel, 5, [2 * rows + 16, 3 * rows + 16, rows], WHOLE_VMEM, keys, values, queries, ids)
+    return kv, kvo, kvq, q
 
 
 def id_row(ref, at):
@@ -229,34 +237,31 @@
     def swap(x):
         return lax.ppermute(x, AXES, [(d, d ^ 1) for d in range(count)])
 
-    def pair_a(x):
-        return lax.ppermute(x, AXES, [(d, d ^ 2) for d in range(count)])
-
-    def pair_b(x):
-        ups = [(2 * c + i, 2 * c + 2 + i) for c in range(1, chips - 1, 2) for i in range(2)]
+    def pair_a(x, cross=0):
+        return lax.ppermute(x, AXES, [(d, d ^ 2 ^ cross) for d in range(count)])
+
+    def pair_b(x, cross=0):
+        ups = [(2 * c + i, 2 * c + 2 + (i ^ cross)) for c in range(1, chips - 1, 2) for i in range(2)]
         return lax.ppermute(x, AXES, ups + [(v, u) for u, v in ups])
 
-    kv, kvq, q = pack(core_arr, queries, key_feats, value_feats, segment_ids.reshape(1, tokens))
+    kv, kvo, kvq, q = pack(core_arr, queries, key_feats, value_feats, segment_ids.reshape(1, tokens))
+    b1 = pair_b(kv)
     a1 = pair_a(kv)
-    b1 = pair_b(kv)
+    b1x = pair_b(kvo, 1)
+    a1x = pair_a(kvo, 1)
     kvq2 = swap(kvq)
-    kv2 = kvq2[: kv.shape[0]]
-    a1b = pair_a(kv2)
-    b1b = pair_b(kv2)
+    b2 = pair_b(a1)
+    a2 = pair_a(b1)
     heads = width // 2 // HD
-    qs, qids = [q, kvq2], [kv, kv2]
-    carry = attend(heads, qs, qids, [kv, kv2], [], False)
-    a1, b1, carry = lax.optimization_barrier((a1, b1, carry))
-    a2 = pair_a(b1)
-    b2 = pair_b(a1)
-    carry = attend(heads, qs, qids, [a1, b1], carry, False)
-    a1b, b1b, carry = lax.optimization_barrier((a1b, b1b, carry))
-    a2b = pair_a(b1b)
-    b2b = pair_b(a1b)
-    carry = attend(heads, qs, qids, [a1b, b1b, a2, b2], carry, False)
-    (o_other,) = attend(heads, [kvq2], [kv2], [a2b, b2b], [carry[1]], True)
+    qs, qids = [q, kvq2], [kv, kvq2]
+    carry = attend(heads, qs, qids, [kv, kvq2, a1, b1], [], False)
+    a1x, b1x, carry = lax.optimization_barrier((a1x, b1x, carry))
+    b2x = pair_b(a1x)
+    a2x = pair_a(b1x)
+    carry = attend(heads, qs, qids, [a1x, b1x, a2, b2], carry, False)
+    (o_other,) = attend(heads, [kvq2], [kvq2], [a2x, b2x], [carry[1]], True)
     back = swap(o_other)
-    (o_mine,) = attend(heads, [q], [kv], [a2b, b2b], [carry[0]], True)
+    (o_mine,) = attend(heads, [q], [kv], [a2x, b2x], [carry[0]], True)
     return place(core_arr, o_mine, back, tokens, width)
 
 

time: 85.5 us -> 86.8 us (1.015)
  waiting for transfers between devices: 15.5 us -> 21 us
  starting transfers between devices: 52.3 us -> 47.2 us
  local copies, waits for them, and re-layouts: 0.05 us -> 1.99 us
  Pallas kernels: 16.7 us -> 15.4 us
    ppermute x4, waiting for transfers between devices: 2.16 us -> 13.1 us  [pair_a(): return lax.ppermute(x, AXES, [(d, d ^ 2 ^ cross) for d in range(count)])]
    ppermute x4, waiting for transfers between devices: 12.7 us -> 7.4 us  [pair_b(): return lax.ppermute(x, AXES, ups + [(v, u) for u, v in ups])]
    ppermute x4, starting transfers between devices: 37.4 us -> 34.3 us  [pair_b(): return lax.ppermute(x, AXES, ups + [(v, u) for u, v in ups])]
    unnamed x4 -> x8, local copies, waits for them, and re-layouts: 0.01 us -> 1.99 us
    ppermute x4, starting transfers between devices: 10.9 us -> 9.11 us  [pair_a(): return lax.ppermute(x, AXES, [(d, d ^ 2 ^ cross) for d in range(count)])]
    pallas_call x5 -> x4, Pallas kernels: 10.3 us -> 8.74 us  [attend(): pl.pallas_call(functools.partial(attend_kernel, heads, tokens, groups, n_...]
  transfers between devices with their start and end apart: 10 -> 10, of which waited for: 5 -> 6; matrix products, arithmetic and copies ran while one was open for 0% -> 0% of each run, Pallas kernels for 11% -> 9%
where the time goes in v2:
time: 86.8 us; the launch traced here: 85.9 us
  starting transfers between devices  47.2 us (54%)
  waiting for transfers between devices  21 us (24%)
  Pallas kernels  15.4 us (18%)
  local copies, waits for them, and re-layouts  1.99 us (2%)
    ppermute x4, starting transfers between devices, pair_b(): return lax.ppermute(x, AXES, ups + [(v, u) for u, v in ups])  34.3 us
    ppermute x4, waiting for transfers between devices, pair_a(): return lax.ppermute(x, AXES, [(d, d ^ 2 ^ cross) for d in range(count)])  13.1 us
    ppermute x4, starting transfers between devices, pair_a(): return lax.ppermute(x, AXES, [(d, d ^ 2 ^ cross) for d in range(count)])  9.11 us
    pallas_call x4, Pallas kernels, attend(): pl.pallas_call(functools.partial(attend_kernel, heads, tokens, groups, n_...  8.74 us
    ppermute x4, waiting for transfers between devices, pair_b(): return lax.ppermute(x, AXES, ups + [(v, u) for u, v in ups])  7.4 us
    pallas_call x2, Pallas kernels, call(): pl.pallas_call(kernel, in_specs=[pl.BlockSpec(memory_space=pltpu.SMEM)] +...  5.75 us
    ppermute x2, starting transfers between devices, swap(): return lax.ppermute(x, AXES, [(d, d ^ 1) for d in range(count)])  3.84 us
    unnamed x8, local copies, waits for them, and re-layouts  1.99 us
  transfers between devices with their start and end apart: 10, of which 6 were waited for; matrix products, arithmetic and copies ran while one was open for 0% of the time, Pallas kernels for 9%

profile of v2, /device:TPU:8, one launch (start us, length us, event | category | flops | bytes accessed | tf_op | source)
XLA Modules:
  0.0 85.9 jit_solution(14024608408731655411)
XLA Ops:
  0.0 2.4 %shard_map.46.refs_2_.refs_4_.refs_1_ = bf16[2064,128]{1,0:T(8,128)(2,1)} custom-call(s32[1]{0:T(128)} %bitcast.core_ref, bf16[128,2048]{1,0:T(8,128)(2,1)} %k_hbm.2, bf16[128,2048]{1,0:T(8,128)(2,1)} %v_hbm.2, s32[1,128]{1,0:T(1,128)} %bitcast.2), custom_call_target="tpu_custom_call" | custom-call | tf_op jit(solution)/shard_map/pallas_call | solution.py:93
  2.5 3.3 %shard_map.47 = (bf16[2064,128]{1,0:T(8,128)(2,1)}, bf16[3088,128]{1,0:T(8,128)(2,1)}, bf16[1024,128]{1,0:T(8,128)(2,1)}) custom-call(s32[1]{0:T(128)} %bitcast.core_ref, bf16[128,2048]{1,0:T(8,128)(2,1)} %k_hbm.2, bf16[128,2048]{1,0:T(8,128)(2,1)} %v_hbm.2, bf16[128,2048]{1,0:T(8,128)(2,1)} %q_hbm, s32[1,128]{1,0:T(1,128)} %bitcast.3), custom_call_target="tpu_custom_call" | custom-call | tf_op jit(solution)/shard_map/pallas_call | solution.py:93
  5.8 1.9 %collective-permute-start.2 = (bf16[3088,128]{1,0:T(8,128)(2,1)}, bf16[3088,128]{1,0:T(8,128)(2,1)S(1)}, u32[]{:S(2)}, u32[]{:S(2)}) collective-permute-start(bf16[3088,128]{1,0:T(8,128)(2,1)} %get-tuple-element.32), channel_id=1, source_target_pairs={{0,1},{1,0},{2,3},{3,2},{4,5},{5,4},{6,7},{7,6},{8,9},{9,8},{10,11... | collective-permute-start | bytes 2371592 | tf_op jit(solution)/shard_map/ppermute | solution.py:238
  7.7 21.0 %collective-permute-start.4 = (bf16[2064,128]{1,0:T(8,128)(2,1)}, bf16[2064,128]{1,0:T(8,128)(2,1)S(1)}, u32[]{:S(2)}, u32[]{:S(2)}) collective-permute-start(bf16[2064,128]{1,0:T(8,128)(2,1)} %shard_map.46.refs_2_.refs_4_.refs_1_), channel_id=1, source_target_pairs={{2,4},{3,5},{6,8},{7,9},{10,12},{11,13},{14,16},{15,17},{18,20},{1... | collective-permute-start | bytes 1585160 | tf_op jit(solution)/shard_map/ppermute | solution.py:245
  28.7 1.9 %collective-permute-start.3 = (bf16[2064,128]{1,0:T(8,128)(2,1)}, bf16[2064,128]{1,0:T(8,128)(2,1)S(1)}, u32[]{:S(2)}, u32[]{:S(2)}) collective-permute-start(bf16[2064,128]{1,0:T(8,128)(2,1)} %shard_map.46.refs_2_.refs_4_.refs_1_), channel_id=1, source_target_pairs={{0,2},{1,3},{2,0},{3,1},{4,6},{5,7},{6,4},{7,5},{8,10},{9,11},{10,... | collective-permute-start | bytes 1585160 | tf_op jit(solution)/shard_map/ppermute | solution.py:241
  30.6 2.0 %collective-permute-start.1 = (bf16[2064,128]{1,0:T(8,128)(2,1)}, bf16[2064,128]{1,0:T(8,128)(2,1)S(1)}, u32[]{:S(2)}, u32[]{:S(2)}) collective-permute-start(bf16[2064,128]{1,0:T(8,128)(2,1)} %get-tuple-element.31), channel_id=1, source_target_pairs={{2,5},{3,4},{6,9},{7,8},{10,13},{11,12},{14,17},{15,16},{18,21},{1... | collective-permute-start | bytes 1585160 | tf_op jit(solution)/shard_map/ppermute | solution.py:245
  32.6 3.4 %collective-permute-start = (bf16[2064,128]{1,0:T(8,128)(2,1)}, bf16[2064,128]{1,0:T(8,128)(2,1)S(1)}, u32[]{:S(2)}, u32[]{:S(2)}) collective-permute-start(bf16[2064,128]{1,0:T(8,128)(2,1)} %get-tuple-element.31), channel_id=1, source_target_pairs={{0,3},{1,2},{2,1},{3,0},{4,7},{5,6},{6,5},{7,4},{8,11},{9,10},{10,... | collective-permute-start | bytes 1585160 | tf_op jit(solution)/shard_map/ppermute | solution.py:241
  36.0 5.7 %collective-permute-done.4.refs_7_ = bf16[2064,128]{1,0:T(8,128)(2,1)S(1)} collective-permute-done((bf16[2064,128]{1,0:T(8,128)(2,1)}, bf16[2064,128]{1,0:T(8,128)(2,1)S(1)}, u32[]{:S(2)}, u32[]{:S(2)}) %collective-permute-start.4) | collective-permute-done | bytes 528416 | tf_op jit(solution)/shard_map/ppermute | solution.py:245
  41.8 1.9 %collective-permute-start.7 = (bf16[2064,128]{1,0:T(8,128)(2,1)S(1)}, bf16[2064,128]{1,0:T(8,128)(2,1)S(1)}, u32[]{:S(2)}, u32[]{:S(2)}) collective-permute-start(bf16[2064,128]{1,0:T(8,128)(2,1)S(1)} %collective-permute-done.4.refs_7_), channel_id=1, source_target_pairs={{0,2},{1,3},{2,0},{3,1},{4,6},{5,7},{6,4},{7,5},{8,10},{9,11},{10,... | collective-permute-start | bytes 1585160 | tf_op jit(solution)/shard_map/ppermute | solution.py:241
  43.7 2.0 %collective-permute-done.3.refs_6_ = bf16[2064,128]{1,0:T(8,128)(2,1)S(1)} collective-permute-done((bf16[2064,128]{1,0:T(8,128)(2,1)}, bf16[2064,128]{1,0:T(8,128)(2,1)S(1)}, u32[]{:S(2)}, u32[]{:S(2)}) %collective-permute-start.3) | collective-permute-done | bytes 528416 | tf_op jit(solution)/shard_map/ppermute | solution.py:241
  45.7 7.3 %collective-permute-start.8 = (bf16[2064,128]{1,0:T(8,128)(2,1)S(1)}, bf16[2064,128]{1,0:T(8,128)(2,1)S(1)}, u32[]{:S(2)}, u32[]{:S(2)}) collective-permute-start(bf16[2064,128]{1,0:T(8,128)(2,1)S(1)} %collective-permute-done.3.refs_6_), channel_id=1, source_target_pairs={{2,4},{3,5},{6,8},{7,9},{10,12},{11,13},{14,16},{15,17},{18,20},{1... | collective-permute-start | bytes 1585160 | tf_op jit(solution)/shard_map/ppermute | solution.py:245
  53.0 0.0 collective-permute-done.2.refs_1_.refs_3_.refs_5_.refs_0_
  53.0 0.0 copy-start
  53.1 1.0 %copy-done = bf16[2064,128]{1,0:T(8,128)(2,1)S(1)} copy-done((bf16[2064,128]{1,0:T(8,128)(2,1)S(1)}, bf16[2064,128]{1,0:T(8,128)(2,1)}, u32[]{:S(2)}) %copy-start) | copy-done | bytes 528408
  54.1 0.0 copy-start.2
  54.1 0.9 %copy-done.2 = bf16[1024,128]{1,0:T(8,128)(2,1)S(1)} copy-done((bf16[1024,128]{1,0:T(8,128)(2,1)S(1)}, bf16[1024,128]{1,0:T(8,128)(2,1)}, u32[]{:S(2)}) %copy-start.2) | copy-done | bytes 262168
  55.0 0.0 copy-start.1
  55.0 0.0 copy-start.3
  55.0 3.4 %shard_map.48 = (f32[1024,128]{1,0:T(8,128)S(1)}, f32[16,128]{1,0:T(8,128)S(1)}, f32[1024,128]{1,0:T(8,128)S(1)}, f32[16,128]{1,0:T(8,128)S(1)}) custom-call(bf16[1024,128]{1,0:T(8,128)(2,1)S(1)} %copy-done.2, bf16[3088,128]{1,0:T(8,128)(2,1)S(1)} %collective-permute-done.2.refs_1_.refs_3_.refs_5_.refs_0_, bf16[2064,128]{1,0:T(8,128)(2,1)S(1)} %copy-done, ...), custom_call_target="tpu_custom_call" | custom-call | flops 536870912 | bytes 4194304 | tf_op jit(solution)/shard_map/pallas_call | solution.py:185
  58.5 0.0 collective-permute-done.1.refs_5_
  58.5 0.0 collective-permute-done.refs_4_
  58.5 1.9 %collective-permute-start.5 = (bf16[2064,128]{1,0:T(8,128)(2,1)S(1)}, bf16[2064,128]{1,0:T(8,128)(2,1)S(1)}, u32[]{:S(2)}, u32[]{:S(2)}) collective-permute-start(bf16[2064,128]{1,0:T(8,128)(2,1)S(1)} %collective-permute-done.1.refs_5_), channel_id=1, source_target_pairs={{0,2},{1,3},{2,0},{3,1},{4,6},{5,7},{6,4},{7,5},{8,10},{9,11},{10,... | collective-permute-start | bytes 1585160 | tf_op jit(solution)/shard_map/ppermute | solution.py:241
  60.4 3.9 %collective-permute-start.6 = (bf16[2064,128]{1,0:T(8,128)(2,1)S(1)}, bf16[2064,128]{1,0:T(8,128)(2,1)S(1)}, u32[]{:S(2)}, u32[]{:S(2)}) collective-permute-start(bf16[2064,128]{1,0:T(8,128)(2,1)S(1)} %collective-permute-done.refs_4_), channel_id=1, source_target_pairs={{2,4},{3,5},{6,8},{7,9},{10,12},{11,13},{14,16},{15,17},{18,20},{1... | collective-permute-start | bytes 1585160 | tf_op jit(solution)/shard_map/ppermute | solution.py:245
  64.4 4.0 %collective-permute-done.7.refs_6_ = bf16[2064,128]{1,0:T(8,128)(2,1)S(1)} collective-permute-done((bf16[2064,128]{1,0:T(8,128)(2,1)S(1)}, bf16[2064,128]{1,0:T(8,128)(2,1)S(1)}, u32[]{:S(2)}, u32[]{:S(2)}) %collective-permute-start.7) | collective-permute-done | bytes 528416 | tf_op jit(solution)/shard_map/ppermute | solution.py:241
  68.3 0.0 collective-permute-done.8.refs_7_
  68.3 0.0 copy-done.1
  68.3 0.0 copy-done.3
  68.3 3.5 %shard_map.49 = (f32[1024,128]{1,0:T(8,128)S(1)}, f32[16,128]{1,0:T(8,128)S(1)}, f32[1024,128]{1,0:T(8,128)S(1)}, f32[16,128]{1,0:T(8,128)S(1)}) custom-call(bf16[1024,128]{1,0:T(8,128)(2,1)S(1)} %copy-done.3, bf16[3088,128]{1,0:T(8,128)(2,1)S(1)} %collective-permute-done.2.refs_1_.refs_3_.refs_5_.refs_0_, bf16[2064,128]{1,0:T(8,128)(2,1)S(1)} %copy-done.1, ...), custom_call_target="tpu_custom_call" | custom-call | flops 536870912 | bytes 4194304 | tf_op jit(solution)/shard_map/pallas_call | solution.py:185
  71.8 7.1 %collective-permute-done.5.refs_2_ = bf16[2064,128]{1,0:T(8,128)(2,1)S(1)} collective-permute-done((bf16[2064,128]{1,0:T(8,128)(2,1)S(1)}, bf16[2064,128]{1,0:T(8,128)(2,1)S(1)}, u32[]{:S(2)}, u32[]{:S(2)}) %collective-permute-start.5) | collective-permute-done | bytes 528416 | tf_op jit(solution)/shard_map/ppermute | solution.py:241
  78.9 1.7 %collective-permute-done.6.refs_3_ = bf16[2064,128]{1,0:T(8,128)(2,1)S(1)} collective-permute-done((bf16[2064,128]{1,0:T(8,128)(2,1)S(1)}, bf16[2064,128]{1,0:T(8,128)(2,1)S(1)}, u32[]{:S(2)}, u32[]{:S(2)}) %collective-permute-start.6) | collective-permute-done | bytes 528416 | tf_op jit(solution)/shard_map/ppermute | solution.py:245
  80.6 0.9 %shard_map.51 = bf16[1024,128]{1,0:T(8,128)(2,1)S(1)} custom-call(bf16[3088,128]{1,0:T(8,128)(2,1)S(1)} %collective-permute-done.2.refs_1_.refs_3_.refs_5_.refs_0_, bf16[3088,128]{1,0:T(8,128)(2,1)S(1)} %collective-permute-done.2.refs_1_.refs_3_.refs_5_.refs_0_, bf16[2064,128]{1,0:T(8,128)(2,1)S(1)} %collective-permute-done.5.refs_2_, ...), custom_call_target="tpu_custom_call" | custom-call | flops 134217728 | bytes 2097152 | tf_op jit(solution)/shard_map/pallas_call | solution.py:185
  81.5 1.9 %collective-permute-start.9 = (bf16[1024,128]{1,0:T(8,128)(2,1)S(1)}, bf16[1024,128]{1,0:T(8,128)(2,1)S(1)}, u32[]{:S(2)}, u32[]{:S(2)}) collective-permute-start(bf16[1024,128]{1,0:T(8,128)(2,1)S(1)} %shard_map.51), channel_id=1, source_target_pairs={{0,1},{1,0},{2,3},{3,2},{4,5},{5,4},{6,7},{7,6},{8,9},{9,8},{10,11... | collective-permute-start | bytes 786440 | tf_op jit(solution)/shard_map/ppermute | solution.py:238
  83.4 0.9 %shard_map.50.o_mine = bf16[1024,128]{1,0:T(8,128)(2,1)S(1)} custom-call(bf16[1024,128]{1,0:T(8,128)(2,1)S(1)} %copy-done.3, bf16[2064,128]{1,0:T(8,128)(2,1)S(1)} %copy-done.1, bf16[2064,128]{1,0:T(8,128)(2,1)S(1)} %collective-permute-done.5.refs_2_, bf16[2064,128]{1,0:T(8,128)(2,1)S(1)} %collective-permute-done.6.refs_3_, ...), custom_call_target="tpu_custom_call" | custom-call | flops 134217728 | bytes 2097152 | tf_op jit(solution)/shard_map/pallas_call | solution.py:185
  84.4 0.6 collective-permute-done.9.o_back
  84.9 0.9 %place.1 = bf16[128,2048]{1,0:T(8,128)(2,1)} custom-call(s32[1]{0:T(128)} %bitcast.core_ref, bf16[1024,128]{1,0:T(8,128)(2,1)S(1)} %shard_map.50.o_mine, bf16[1024,128]{1,0:T(8,128)(2,1)S(1)} %collective-permute-done.9.o_back), custom_call_target="tpu_custom_call" | custom-call | tf_op jit(solution)/shard_map/place/pallas_call | solution.py:219
Async XLA Ops:
  5.8 47.3 %collective-permute-start.2 = (bf16[3088,128]{1,0:T(8,128)(2,1)}, bf16[3088,128]{1,0:T(8,128)(2,1)S(1)}, u32[]{:S(2)}, u32[]{:S(2)}) collective-permute-start(bf16[3088,128]{1,0:T(8,128)(2,1)} %get-tuple-element.32), channel_id=1, source_target_pairs={{0,1},{1,0},{2,3},{3,2},{4,5},{5,4},{6,7},{7,6},{8,9},{9,8},{10,11... | collective-permute-start | bytes 2371592 | tf_op jit(solution)/shard_map/ppermute | solution.py:238
  7.7 34.1 %collective-permute-start.4 = (bf16[2064,128]{1,0:T(8,128)(2,1)}, bf16[2064,128]{1,0:T(8,128)(2,1)S(1)}, u32[]{:S(2)}, u32[]{:S(2)}) collective-permute-start(bf16[2064,128]{1,0:T(8,128)(2,1)} %shard_map.46.refs_2_.refs_4_.refs_1_), channel_id=1, source_target_pairs={{2,4},{3,5},{6,8},{7,9},{10,12},{11,13},{14,16},{15,17},{18,20},{1... | collective-permute-start | bytes 1585160 | tf_op jit(solution)/shard_map/ppermute | solution.py:245
  28.7 17.0 %collective-permute-start.3 = (bf16[2064,128]{1,0:T(8,128)(2,1)}, bf16[2064,128]{1,0:T(8,128)(2,1)S(1)}, u32[]{:S(2)}, u32[]{:S(2)}) collective-permute-start(bf16[2064,128]{1,0:T(8,128)(2,1)} %shard_map.46.refs_2_.refs_4_.refs_1_), channel_id=1, source_target_pairs={{0,2},{1,3},{2,0},{3,1},{4,6},{5,7},{6,4},{7,5},{8,10},{9,11},{10,... | collective-permute-start | bytes 1585160 | tf_op jit(solution)/shard_map/ppermute | solution.py:241
  30.6 27.9 %collective-permute-start.1 = (bf16[2064,128]{1,0:T(8,128)(2,1)}, bf16[2064,128]{1,0:T(8,128)(2,1)S(1)}, u32[]{:S(2)}, u32[]{:S(2)}) collective-permute-start(bf16[2064,128]{1,0:T(8,128)(2,1)} %get-tuple-element.31), channel_id=1, source_target_pairs={{2,5},{3,4},{6,9},{7,8},{10,13},{11,12},{14,17},{15,16},{18,21},{1... | collective-permute-start | bytes 1585160 | tf_op jit(solution)/shard_map/ppermute | solution.py:245
  32.6 25.8 %collective-permute-start = (bf16[2064,128]{1,0:T(8,128)(2,1)}, bf16[2064,128]{1,0:T(8,128)(2,1)S(1)}, u32[]{:S(2)}, u32[]{:S(2)}) collective-permute-start(bf16[2064,128]{1,0:T(8,128)(2,1)} %get-tuple-element.31), channel_id=1, source_target_pairs={{0,3},{1,2},{2,1},{3,0},{4,7},{5,6},{6,5},{7,4},{8,11},{9,10},{10,... | collective-permute-start | bytes 1585160 | tf_op jit(solution)/shard_map/ppermute | solution.py:241
  41.8 26.6 %collective-permute-start.7 = (bf16[2064,128]{1,0:T(8,128)(2,1)S(1)}, bf16[2064,128]{1,0:T(8,128)(2,1)S(1)}, u32[]{:S(2)}, u32[]{:S(2)}) collective-permute-start(bf16[2064,128]{1,0:T(8,128)(2,1)S(1)} %collective-permute-done.4.refs_7_), channel_id=1, source_target_pairs={{0,2},{1,3},{2,0},{3,1},{4,6},{5,7},{6,4},{7,5},{8,10},{9,11},{10,... | collective-permute-start | bytes 1585160 | tf_op jit(solution)/shard_map/ppermute | solution.py:241
  45.7 22.6 %collective-permute-start.8 = (bf16[2064,128]{1,0:T(8,128)(2,1)S(1)}, bf16[2064,128]{1,0:T(8,128)(2,1)S(1)}, u32[]{:S(2)}, u32[]{:S(2)}) collective-permute-start(bf16[2064,128]{1,0:T(8,128)(2,1)S(1)} %collective-permute-done.3.refs_6_), channel_id=1, source_target_pairs={{2,4},{3,5},{6,8},{7,9},{10,12},{11,13},{14,16},{15,17},{18,20},{1... | collective-permute-start | bytes 1585160 | tf_op jit(solution)/shard_map/ppermute | solution.py:245
  53.0 1.0 %copy-start = (bf16[2064,128]{1,0:T(8,128)(2,1)S(1)}, bf16[2064,128]{1,0:T(8,128)(2,1)}, u32[]{:S(2)}) copy-start(bf16[2064,128]{1,0:T(8,128)(2,1)} %shard_map.46.refs_2_.refs_4_.refs_1_) | copy-start | bytes 1585156
  54.1 0.9 %copy-start.2 = (bf16[1024,128]{1,0:T(8,128)(2,1)S(1)}, bf16[1024,128]{1,0:T(8,128)(2,1)}, u32[]{:S(2)}) copy-start(bf16[1024,128]{1,0:T(8,128)(2,1)} %get-tuple-element.29.refs_0_) | copy-start | bytes 786436
  55.0 13.3 %copy-start.1 = (bf16[2064,128]{1,0:T(8,128)(2,1)S(1)}, bf16[2064,128]{1,0:T(8,128)(2,1)}, u32[]{:S(2)}) copy-start(bf16[2064,128]{1,0:T(8,128)(2,1)} %shard_map.46.refs_2_.refs_4_.refs_1_) | copy-start | bytes 1585156
  55.0 13.3 %copy-start.3 = (bf16[1024,128]{1,0:T(8,128)(2,1)S(1)}, bf16[1024,128]{1,0:T(8,128)(2,1)}, u32[]{:S(2)}) copy-start(bf16[1024,128]{1,0:T(8,128)(2,1)} %get-tuple-element.29.refs_0_) | copy-start | bytes 786436
  58.5 20.4 %collective-permute-start.5 = (bf16[2064,128]{1,0:T(8,128)(2,1)S(1)}, bf16[2064,128]{1,0:T(8,128)(2,1)S(1)}, u32[]{:S(2)}, u32[]{:S(2)}) collective-permute-start(bf16[2064,128]{1,0:T(8,128)(2,1)S(1)} %collective-permute-done.1.refs_5_), channel_id=1, source_target_pairs={{0,2},{1,3},{2,0},{3,1},{4,6},{5,7},{6,4},{7,5},{8,10},{9,11},{10,... | collective-permute-start | bytes 1585160 | tf_op jit(solution)/shard_map/ppermute | solution.py:241
  60.4 20.1 %collective-permute-start.6 = (bf16[2064,128]{1,0:T(8,128)(2,1)S(1)}, bf16[2064,128]{1,0:T(8,128)(2,1)S(1)}, u32[]{:S(2)}, u32[]{:S(2)}) collective-permute-start(bf16[2064,128]{1,0:T(8,128)(2,1)S(1)} %collective-permute-done.refs_4_), channel_id=1, source_target_pairs={{2,4},{3,5},{6,8},{7,9},{10,12},{11,13},{14,16},{15,17},{18,20},{1... | collective-permute-start | bytes 1585160 | tf_op jit(solution)/shard_map/ppermute | solution.py:245
  81.5 3.4 %collective-permute-start.9 = (bf16[1024,128]{1,0:T(8,128)(2,1)S(1)}, bf16[1024,128]{1,0:T(8,128)(2,1)S(1)}, u32[]{:S(2)}, u32[]{:S(2)}) collective-permute-start(bf16[1024,128]{1,0:T(8,128)(2,1)S(1)} %shard_map.51), channel_id=1, source_target_pairs={{0,1},{1,0},{2,3},{3,2},{4,5},{5,4},{6,7},{7,6},{8,9},{9,8},{10,11... | collective-permute-start | bytes 786440 | tf_op jit(solution)/shard_map/ppermute | solution.py:238

commit v3 on v2

--- a/solution.py
+++ b/solution.py
@@ -13,7 +13,6 @@
 AXES = ("blk", "head")
 NEG = -1e30
 VMEM_LIMIT = 16 << 20
-WHOLE_VMEM = 67043328
 F32 = jnp.float32
 BF16 = jnp.bfloat16
 
@@ -104,9 +103,10 @@
             compiler_params=pltpu.CompilerParams(vmem_limit_bytes=limit),
         )(core, *args)
 
-    (kv,) = call(pack_mine_kernel, 2, [2 * rows + 16], WHOLE_VMEM, keys, values, ids)
+    keys, values, queries, ids = (pltpu.with_memory_space_constraint(x, pltpu.HBM) for x in (keys, values, queries, ids))
+    (kv,) = call(pack_mine_kernel, 2, [2 * rows + 16], VMEM_LIMIT, keys, values, ids)
     keys, values, queries, kv = lax.optimization_barrier((keys, values, queries, kv))
-    kvo, kvq, q = call(pack_other_kernel, 5, [2 * rows + 16, 3 * rows + 16, rows], WHOLE_VMEM, keys, values, queries, ids)
+    kvo, kvq, q = call(pack_other_kernel, 5, [2 * rows + 16, 3 * rows + 16, rows], VMEM_LIMIT, keys, values, queries, ids)
     return kv, kvo, kvq, q
 
 
@@ -254,10 +254,9 @@
     a2 = pair_a(b1)
     heads = width // 2 // HD
     qs, qids = [q, kvq2], [kv, kvq2]
-    carry = attend(heads, qs, qids, [kv, kvq2, a1, b1], [], False)
-    a1x, b1x, carry = lax.optimization_barrier((a1x, b1x, carry))
     b2x = pair_b(a1x)
     a2x = pair_a(b1x)
+    carry = attend(heads, qs, qids, [kv, kvq2, a1, b1], [], False)
     carry = attend(heads, qs, qids, [a1x, b1x, a2, b2], carry, False)
     (o_other,) = attend(heads, [kvq2], [kvq2], [a2x, b2x], [carry[1]], True)
     back = swap(o_other)

time: 86.8 us -> 79 us (0.910)
  the two profiles are of different devices: /device:TPU:8 before, /device:TPU:15 now
where the time goes in v3:
time: 79 us; the launch traced here: 78.5 us
  starting transfers between devices  52.1 us (66%)
  Pallas kernels  13.5 us (17%)
  waiting for transfers between devices  12.8 us (16%)
    ppermute x4, starting transfers between devices, pair_b(): return lax.ppermute(x, AXES, ups + [(v, u) for u, v in ups])  36.6 us
    ppermute x4, waiting for transfers between devices, pair_a(): return lax.ppermute(x, AXES, [(d, d ^ 2 ^ cross) for d in range(count)])  10.1 us
    ppermute x4, starting transfers between devices, pair_a(): return lax.ppermute(x, AXES, [(d, d ^ 2 ^ cross) for d in range(count)])  9.77 us
    pallas_call x4, Pallas kernels, attend(): pl.pallas_call(functools.partial(attend_kernel, heads, tokens, groups, n_...  8.75 us
    ppermute x2, starting transfers between devices, swap(): return lax.ppermute(x, AXES, [(d, d ^ 1) for d in range(count)])  5.64 us
    pallas_call x2, Pallas kernels, call(): pl.pallas_call(kernel, in_specs=[pl.BlockSpec(memory_space=pltpu.SMEM)] +...  3.82 us
    ppermute x4, waiting for transfers between devices, pair_b(): return lax.ppermute(x, AXES, ups + [(v, u) for u, v in ups])  2.47 us
  transfers between devices with their start and end apart: 10, of which 5 were waited for; matrix products, arithmetic and copies ran while one was open for 0% of the time, Pallas kernels for 13%

profile of v3, /device:TPU:15, one launch (start us, length us, event | category | flops | bytes accessed | tf_op | source)
XLA Modules:
  0.0 78.5 jit_solution(9193873552885603534)
XLA Ops:
  0.0 1.6 %shard_map.46.refs_2_.refs_4_.refs_1_ = bf16[2064,128]{1,0:T(8,128)(2,1)S(1)} custom-call(s32[1]{0:T(128)} %bitcast.core_ref, bf16[128,2048]{1,0:T(8,128)(2,1)} %k_hbm.2, bf16[128,2048]{1,0:T(8,128)(2,1)} %v_hbm.2, s32[1,128]{1,0:T(1,128)} %bitcast.2), custom_call_target="tpu_custom_call" | custom-call | tf_op jit(solution)/shard_map/pallas_call | solution.py:92
  1.7 21.6 %collective-permute-start.5 = (bf16[2064,128]{1,0:T(8,128)(2,1)S(1)}, bf16[2064,128]{1,0:T(8,128)(2,1)S(1)}, u32[]{:S(2)}, u32[]{:S(2)}) collective-permute-start(bf16[2064,128]{1,0:T(8,128)(2,1)S(1)} %shard_map.46.refs_2_.refs_4_.refs_1_), channel_id=1, source_target_pairs={{2,4},{3,5},{6,8},{7,9},{10,12},{11,13},{14,16},{15,17},{18,20},{1... | collective-permute-start | bytes 1585160 | tf_op jit(solution)/shard_map/ppermute | solution.py:245
  23.3 1.9 %collective-permute-start.7 = (bf16[2064,128]{1,0:T(8,128)(2,1)S(1)}, bf16[2064,128]{1,0:T(8,128)(2,1)S(1)}, u32[]{:S(2)}, u32[]{:S(2)}) collective-permute-start(bf16[2064,128]{1,0:T(8,128)(2,1)S(1)} %shard_map.46.refs_2_.refs_4_.refs_1_), channel_id=1, source_target_pairs={{0,2},{1,3},{2,0},{3,1},{4,6},{5,7},{6,4},{7,5},{8,10},{9,11},{10,... | collective-permute-start | bytes 1585160 | tf_op jit(solution)/shard_map/ppermute | solution.py:241
  25.2 2.2 %shard_map.47 = (bf16[2064,128]{1,0:T(8,128)(2,1)S(1)}, bf16[3088,128]{1,0:T(8,128)(2,1)S(1)}, bf16[1024,128]{1,0:T(8,128)(2,1)S(1)}) custom-call(s32[1]{0:T(128)} %bitcast.core_ref, bf16[128,2048]{1,0:T(8,128)(2,1)} %k_hbm.2, bf16[128,2048]{1,0:T(8,128)(2,1)} %v_hbm.2, bf16[128,2048]{1,0:T(8,128)(2,1)} %q_hbm, s32[1,128]{1,0:T(1,128)} %bitcast.3), custom_call_target="tpu_custom_call" | custom-call | tf_op jit(solution)/shard_map/pallas_call | solution.py:92
  27.4 2.5 %collective-permute-start = (bf16[2064,128]{1,0:T(8,128)(2,1)S(1)}, bf16[2064,128]{1,0:T(8,128)(2,1)S(1)}, u32[]{:S(2)}, u32[]{:S(2)}) collective-permute-start(bf16[2064,128]{1,0:T(8,128)(2,1)S(1)} %get-tuple-element.25), channel_id=1, source_target_pairs={{2,5},{3,4},{6,9},{7,8},{10,13},{11,12},{14,17},{15,16},{18,21},{1... | collective-permute-start | bytes 1585160 | tf_op jit(solution)/shard_map/ppermute | solution.py:245
  29.9 3.9 %collective-permute-start.2 = (bf16[2064,128]{1,0:T(8,128)(2,1)S(1)}, bf16[2064,128]{1,0:T(8,128)(2,1)S(1)}, u32[]{:S(2)}, u32[]{:S(2)}) collective-permute-start(bf16[2064,128]{1,0:T(8,128)(2,1)S(1)} %get-tuple-element.25), channel_id=1, source_target_pairs={{0,3},{1,2},{2,1},{3,0},{4,7},{5,6},{6,5},{7,4},{8,11},{9,10},{10,... | collective-permute-start | bytes 1585160 | tf_op jit(solution)/shard_map/ppermute | solution.py:241
  33.8 1.9 %collective-permute-start.4 = (bf16[3088,128]{1,0:T(8,128)(2,1)S(1)}, bf16[3088,128]{1,0:T(8,128)(2,1)S(1)}, u32[]{:S(2)}, u32[]{:S(2)}) collective-permute-start(bf16[3088,128]{1,0:T(8,128)(2,1)S(1)} %get-tuple-element.26), channel_id=1, source_target_pairs={{0,1},{1,0},{2,3},{3,2},{4,5},{5,4},{6,7},{7,6},{8,9},{9,8},{10,11... | collective-permute-start | bytes 2371592 | tf_op jit(solution)/shard_map/ppermute | solution.py:238
  35.7 0.0 collective-permute-done.5.refs_7_
  35.7 2.0 %collective-permute-start.6 = (bf16[2064,128]{1,0:T(8,128)(2,1)S(1)}, bf16[2064,128]{1,0:T(8,128)(2,1)S(1)}, u32[]{:S(2)}, u32[]{:S(2)}) collective-permute-start(bf16[2064,128]{1,0:T(8,128)(2,1)S(1)} %collective-permute-done.5.refs_7_), channel_id=1, source_target_pairs={{0,2},{1,3},{2,0},{3,1},{4,6},{5,7},{6,4},{7,5},{8,10},{9,11},{10,... | collective-permute-start | bytes 1585160 | tf_op jit(solution)/shard_map/ppermute | solution.py:241
  37.8 0.0 collective-permute-done.7.refs_6_
  37.8 7.6 %collective-permute-start.8 = (bf16[2064,128]{1,0:T(8,128)(2,1)S(1)}, bf16[2064,128]{1,0:T(8,128)(2,1)S(1)}, u32[]{:S(2)}, u32[]{:S(2)}) collective-permute-start(bf16[2064,128]{1,0:T(8,128)(2,1)S(1)} %collective-permute-done.7.refs_6_), channel_id=1, source_target_pairs={{2,4},{3,5},{6,8},{7,9},{10,12},{11,13},{14,16},{15,17},{18,20},{1... | collective-permute-start | bytes 1585160 | tf_op jit(solution)/shard_map/ppermute | solution.py:245
  45.4 2.5 %collective-permute-done.refs_5_ = bf16[2064,128]{1,0:T(8,128)(2,1)S(1)} collective-permute-done((bf16[2064,128]{1,0:T(8,128)(2,1)S(1)}, bf16[2064,128]{1,0:T(8,128)(2,1)S(1)}, u32[]{:S(2)}, u32[]{:S(2)}) %collective-permute-start) | collective-permute-done | bytes 528416 | tf_op jit(solution)/shard_map/ppermute | solution.py:245
  47.8 1.9 %collective-permute-start.1 = (bf16[2064,128]{1,0:T(8,128)(2,1)S(1)}, bf16[2064,128]{1,0:T(8,128)(2,1)S(1)}, u32[]{:S(2)}, u32[]{:S(2)}) collective-permute-start(bf16[2064,128]{1,0:T(8,128)(2,1)S(1)} %collective-permute-done.refs_5_), channel_id=1, source_target_pairs={{0,2},{1,3},{2,0},{3,1},{4,6},{5,7},{6,4},{7,5},{8,10},{9,11},{10,... | collective-permute-start | bytes 1585160 | tf_op jit(solution)/shard_map/ppermute | solution.py:241
  49.7 2.2 %collective-permute-done.2.refs_4_ = bf16[2064,128]{1,0:T(8,128)(2,1)S(1)} collective-permute-done((bf16[2064,128]{1,0:T(8,128)(2,1)S(1)}, bf16[2064,128]{1,0:T(8,128)(2,1)S(1)}, u32[]{:S(2)}, u32[]{:S(2)}) %collective-permute-start.2) | collective-permute-done | bytes 528416 | tf_op jit(solution)/shard_map/ppermute | solution.py:241
  51.9 5.0 %collective-permute-start.3 = (bf16[2064,128]{1,0:T(8,128)(2,1)S(1)}, bf16[2064,128]{1,0:T(8,128)(2,1)S(1)}, u32[]{:S(2)}, u32[]{:S(2)}) collective-permute-start(bf16[2064,128]{1,0:T(8,128)(2,1)S(1)} %collective-permute-done.2.refs_4_), channel_id=1, source_target_pairs={{2,4},{3,5},{6,8},{7,9},{10,12},{11,13},{14,16},{15,17},{18,20},{1... | collective-permute-start | bytes 1585160 | tf_op jit(solution)/shard_map/ppermute | solution.py:245
  56.9 0.0 collective-permute-done.4.refs_1_.refs_3_.refs_5_.refs_0_
  56.9 3.4 %shard_map.48 = (f32[1024,128]{1,0:T(8,128)S(1)}, f32[16,128]{1,0:T(8,128)S(1)}, f32[1024,128]{1,0:T(8,128)S(1)}, f32[16,128]{1,0:T(8,128)S(1)}) custom-call(bf16[1024,128]{1,0:T(8,128)(2,1)S(1)} %get-tuple-element.23.refs_0_, bf16[3088,128]{1,0:T(8,128)(2,1)S(1)} %collective-permute-done.4.refs_1_.refs_3_.refs_5_.refs_0_, ...), custom_call_target="tpu_custom_call" | custom-call | flops 536870912 | bytes 4194304 | tf_op jit(solution)/shard_map/pallas_call | solution.py:185
  60.4 0.1 collective-permute-done.6.refs_6_
  60.4 0.0 collective-permute-done.8.refs_7_
  60.4 3.5 %shard_map.49 = (f32[1024,128]{1,0:T(8,128)S(1)}, f32[16,128]{1,0:T(8,128)S(1)}, f32[1024,128]{1,0:T(8,128)S(1)}, f32[16,128]{1,0:T(8,128)S(1)}) custom-call(bf16[1024,128]{1,0:T(8,128)(2,1)S(1)} %get-tuple-element.23.refs_0_, bf16[3088,128]{1,0:T(8,128)(2,1)S(1)} %collective-permute-done.4.refs_1_.refs_3_.refs_5_.refs_0_, ...), custom_call_target="tpu_custom_call" | custom-call | flops 536870912 | bytes 4194304 | tf_op jit(solution)/shard_map/pallas_call | solution.py:185
  63.9 7.9 %collective-permute-done.1.refs_2_ = bf16[2064,128]{1,0:T(8,128)(2,1)S(1)} collective-permute-done((bf16[2064,128]{1,0:T(8,128)(2,1)S(1)}, bf16[2064,128]{1,0:T(8,128)(2,1)S(1)}, u32[]{:S(2)}, u32[]{:S(2)}) %collective-permute-start.1) | collective-permute-done | bytes 528416 | tf_op jit(solution)/shard_map/ppermute | solution.py:241
  71.7 0.0 collective-permute-done.3.refs_3_
  71.7 0.9 %shard_map.51 = bf16[1024,128]{1,0:T(8,128)(2,1)S(1)} custom-call(bf16[3088,128]{1,0:T(8,128)(2,1)S(1)} %collective-permute-done.4.refs_1_.refs_3_.refs_5_.refs_0_, bf16[3088,128]{1,0:T(8,128)(2,1)S(1)} %collective-permute-done.4.refs_1_.refs_3_.refs_5_.refs_0_, bf16[2064,128]{1,0:T(8,128)(2,1)S(1)} %collective-permute-done.1.refs_2_, ...), custom_call_target="tpu_custom_call" | custom-call | flops 134217728 | bytes 2097152 | tf_op jit(solution)/shard_map/pallas_call | solution.py:185
  72.7 3.7 %collective-permute-start.9 = (bf16[1024,128]{1,0:T(8,128)(2,1)S(1)}, bf16[1024,128]{1,0:T(8,128)(2,1)S(1)}, u32[]{:S(2)}, u32[]{:S(2)}) collective-permute-start(bf16[1024,128]{1,0:T(8,128)(2,1)S(1)} %shard_map.51), channel_id=1, source_target_pairs={{0,1},{1,0},{2,3},{3,2},{4,5},{5,4},{6,7},{7,6},{8,9},{9,8},{10,11... | collective-permute-start | bytes 786440 | tf_op jit(solution)/shard_map/ppermute | solution.py:238
  76.4 0.9 %shard_map.50.o_mine = bf16[1024,128]{1,0:T(8,128)(2,1)S(1)} custom-call(bf16[1024,128]{1,0:T(8,128)(2,1)S(1)} %get-tuple-element.23.refs_0_, bf16[2064,128]{1,0:T(8,128)(2,1)S(1)} %shard_map.46.refs_2_.refs_4_.refs_1_, bf16[2064,128]{1,0:T(8,128)(2,1)S(1)} %collective-permute-done.1.refs_2_, bf16[2064,128]{1,0:T(8,128)(2,1)S(1)} %collective-permute-done.3.refs_3_, ...), custom_call_target="tpu_custom_call" | custom-call | flops 134217728 | bytes 2097152 | tf_op jit(solution)/shard_map/pallas_call | solution.py:185
  77.3 0.2 collective-permute-done.9.o_back
  77.5 0.9 %place.1 = bf16[128,2048]{1,0:T(8,128)(2,1)} custom-call(s32[1]{0:T(128)} %bitcast.core_ref, bf16[1024,128]{1,0:T(8,128)(2,1)S(1)} %shard_map.50.o_mine, bf16[1024,128]{1,0:T(8,128)(2,1)S(1)} %collective-permute-done.9.o_back), custom_call_target="tpu_custom_call" | custom-call | tf_op jit(solution)/shard_map/place/pallas_call | solution.py:219
Async XLA Ops:
  1.7 34.1 %collective-permute-start.5 = (bf16[2064,128]{1,0:T(8,128)(2,1)S(1)}, bf16[2064,128]{1,0:T(8,128)(2,1)S(1)}, u32[]{:S(2)}, u32[]{:S(2)}) collective-permute-start(bf16[2064,128]{1,0:T(8,128)(2,1)S(1)} %shard_map.46.refs_2_.refs_4_.refs_1_), channel_id=1, source_target_pairs={{2,4},{3,5},{6,8},{7,9},{10,12},{11,13},{14,16},{15,17},{18,20},{1... | collective-permute-start | bytes 1585160 | tf_op jit(solution)/shard_map/ppermute | solution.py:245
  23.3 14.5 %collective-permute-start.7 = (bf16[2064,128]{1,0:T(8,128)(2,1)S(1)}, bf16[2064,128]{1,0:T(8,128)(2,1)S(1)}, u32[]{:S(2)}, u32[]{:S(2)}) collective-permute-start(bf16[2064,128]{1,0:T(8,128)(2,1)S(1)} %shard_map.46.refs_2_.refs_4_.refs_1_), channel_id=1, source_target_pairs={{0,2},{1,3},{2,0},{3,1},{4,6},{5,7},{6,4},{7,5},{8,10},{9,11},{10,... | collective-permute-start | bytes 1585160 | tf_op jit(solution)/shard_map/ppermute | solution.py:241
  27.4 20.5 %collective-permute-start = (bf16[2064,128]{1,0:T(8,128)(2,1)S(1)}, bf16[2064,128]{1,0:T(8,128)(2,1)S(1)}, u32[]{:S(2)}, u32[]{:S(2)}) collective-permute-start(bf16[2064,128]{1,0:T(8,128)(2,1)S(1)} %get-tuple-element.25), channel_id=1, source_target_pairs={{2,5},{3,4},{6,9},{7,8},{10,13},{11,12},{14,17},{15,16},{18,21},{1... | collective-permute-start | bytes 1585160 | tf_op jit(solution)/shard_map/ppermute | solution.py:245
  29.9 22.1 %collective-permute-start.2 = (bf16[2064,128]{1,0:T(8,128)(2,1)S(1)}, bf16[2064,128]{1,0:T(8,128)(2,1)S(1)}, u32[]{:S(2)}, u32[]{:S(2)}) collective-permute-start(bf16[2064,128]{1,0:T(8,128)(2,1)S(1)} %get-tuple-element.25), channel_id=1, source_target_pairs={{0,3},{1,2},{2,1},{3,0},{4,7},{5,6},{6,5},{7,4},{8,11},{9,10},{10,... | collective-permute-start | bytes 1585160 | tf_op jit(solution)/shard_map/ppermute | solution.py:241
  33.8 23.1 %collective-permute-start.4 = (bf16[3088,128]{1,0:T(8,128)(2,1)S(1)}, bf16[3088,128]{1,0:T(8,128)(2,1)S(1)}, u32[]{:S(2)}, u32[]{:S(2)}) collective-permute-start(bf16[3088,128]{1,0:T(8,128)(2,1)S(1)} %get-tuple-element.26), channel_id=1, source_target_pairs={{0,1},{1,0},{2,3},{3,2},{4,5},{5,4},{6,7},{7,6},{8,9},{9,8},{10,11... | collective-permute-start | bytes 2371592 | tf_op jit(solution)/shard_map/ppermute | solution.py:238
  35.7 24.7 %collective-permute-start.6 = (bf16[2064,128]{1,0:T(8,128)(2,1)S(1)}, bf16[2064,128]{1,0:T(8,128)(2,1)S(1)}, u32[]{:S(2)}, u32[]{:S(2)}) collective-permute-start(bf16[2064,128]{1,0:T(8,128)(2,1)S(1)} %collective-permute-done.5.refs_7_), channel_id=1, source_target_pairs={{0,2},{1,3},{2,0},{3,1},{4,6},{5,7},{6,4},{7,5},{8,10},{9,11},{10,... | collective-permute-start | bytes 1585160 | tf_op jit(solution)/shard_map/ppermute | solution.py:241
  37.8 22.6 %collective-permute-start.8 = (bf16[2064,128]{1,0:T(8,128)(2,1)S(1)}, bf16[2064,128]{1,0:T(8,128)(2,1)S(1)}, u32[]{:S(2)}, u32[]{:S(2)}) collective-permute-start(bf16[2064,128]{1,0:T(8,128)(2,1)S(1)} %collective-permute-done.7.refs_6_), channel_id=1, source_target_pairs={{2,4},{3,5},{6,8},{7,9},{10,12},{11,13},{14,16},{15,17},{18,20},{1... | collective-permute-start | bytes 1585160 | tf_op jit(solution)/shard_map/ppermute | solution.py:245
  47.8 23.9 %collective-permute-start.1 = (bf16[2064,128]{1,0:T(8,128)(2,1)S(1)}, bf16[2064,128]{1,0:T(8,128)(2,1)S(1)}, u32[]{:S(2)}, u32[]{:S(2)}) collective-permute-start(bf16[2064,128]{1,0:T(8,128)(2,1)S(1)} %collective-permute-done.refs_5_), channel_id=1, source_target_pairs={{0,2},{1,3},{2,0},{3,1},{4,6},{5,7},{6,4},{7,5},{8,10},{9,11},{10,... | collective-permute-start | bytes 1585160 | tf_op jit(solution)/shard_map/ppermute | solution.py:241
  51.9 19.8 %collective-permute-start.3 = (bf16[2064,128]{1,0:T(8,128)(2,1)S(1)}, bf16[2064,128]{1,0:T(8,128)(2,1)S(1)}, u32[]{:S(2)}, u32[]{:S(2)}) collective-permute-start(bf16[2064,128]{1,0:T(8,128)(2,1)S(1)} %collective-permute-done.2.refs_4_), channel_id=1, source_target_pairs={{2,4},{3,5},{6,8},{7,9},{10,12},{11,13},{14,16},{15,17},{18,20},{1... | collective-permute-start | bytes 1585160 | tf_op jit(solution)/shard_map/ppermute | solution.py:245
  72.7 4.9 %collective-permute-start.9 = (bf16[1024,128]{1,0:T(8,128)(2,1)S(1)}, bf16[1024,128]{1,0:T(8,128)(2,1)S(1)}, u32[]{:S(2)}, u32[]{:S(2)}) collective-permute-start(bf16[1024,128]{1,0:T(8,128)(2,1)S(1)} %shard_map.51), channel_id=1, source_target_pairs={{0,1},{1,0},{2,3},{3,2},{4,5},{5,4},{6,7},{7,6},{8,9},{9,8},{10,11... | collective-permute-start | bytes 786440 | tf_op jit(solution)/shard_map/ppermute | solution.py:238

commit v4 on v3

--- a/solution.py
+++ b/solution.py
@@ -115,8 +115,9 @@
     return tile[0:1, :] * 16.0 + tile[1:2, :]
 
 
-def attend_kernel(heads, tokens, groups, n_buf, first, last, *refs):
+def attend_kernel(heads, tokens, groups, n_buf, first, last, direct, *refs):
     refs = list(refs)
+    core = refs.pop(0)[0] if direct else None
     qs = [refs.pop(0) for _ in range(groups)]
     qids = [refs.pop(0) for _ in range(groups)]
     bufs = [refs.pop(0) for _ in range(n_buf)]
@@ -126,6 +127,9 @@
     else:
         outs = [(refs.pop(0), refs.pop(0)) for _ in range(groups)]
     bias = refs.pop(0)
+    if direct:
+        o_buf, sems = refs
+        copies = []
     full = heads * tokens
     at = 2 * full
     scale = 1.0 / (math.sqrt(HD) * math.log(2.0))
@@ -162,16 +166,29 @@
             acc = acc * (1.0 / l)
         for g in range(groups):
             lanes = slice(g * tokens, (g + 1) * tokens)
-            if last:
+            if direct:
+                o_buf[rows, :] = acc[:, lanes].T.astype(BF16)
+                copies.append(put_head(o_buf, rows, outs[g], core, head, sems))
+            elif last:
                 outs[g][rows, :] = acc[:, lanes].T.astype(BF16)
             else:
                 new_acc, new_stat = outs[g]
                 new_acc[rows, :] = acc[:, lanes]
                 new_stat[head : head + 1, :] = m[:, lanes]
                 new_stat[heads + head : heads + head + 1, :] = l[:, lanes]
-
-
-def attend(heads, qs, qids, bufs, carry, last):
+    if direct:
+        for copy in copies:
+            copy.wait()
+
+
+def put_head(source, rows, out_ref, side, head, sems):
+    first_col = pl.multiple_of(side * (out_ref.shape[1] // 2) + head * HD, HD)
+    copy = pltpu.make_async_copy(source.at[rows, :], out_ref.at[:, pl.ds(first_col, HD)], sems.at[head])
+    copy.start()
+    return copy
+
+
+def attend(heads, qs, qids, bufs, carry, last, direct=None):
     groups, n_buf, tokens = len(qs), len(bufs), HD
     rows = heads * tokens
     first = not carry
@@ -181,49 +198,52 @@
     else:
         shapes = [jax.ShapeDtypeStruct((n, tokens), F32) for _ in range(groups) for n in (rows, 2 * heads)]
     vmem = pl.BlockSpec(memory_space=pltpu.VMEM)
+    first_specs, out_specs, more_scratch, first_args = [], [vmem] * len(shapes), [], ()
+    if direct is not None:
+        shapes = [jax.ShapeDtypeStruct((tokens, 2 * rows), BF16)]
+        first_specs, out_specs = [pl.BlockSpec(memory_space=pltpu.SMEM)], [pl.BlockSpec(memory_space=pltpu.HBM)]
+        more_scratch = [pltpu.VMEM((rows, HD), BF16), pltpu.SemaphoreType.DMA((heads,))]
+        first_args = (direct,)
     elements = groups * rows * n_buf * tokens
     out = pl.pallas_call(
-        functools.partial(attend_kernel, heads, tokens, groups, n_buf, first, last),
-        in_specs=[vmem] * (2 * groups + n_buf + len(flat_carry)),
-        out_specs=[vmem] * len(shapes),
+        functools.partial(attend_kernel, heads, tokens, groups, n_buf, first, last, direct is not None),
+        in_specs=first_specs + [vmem] * (2 * groups + n_buf + len(flat_carry)),
+        out_specs=out_specs,
         out_shape=shapes,
-        scratch_shapes=[pltpu.VMEM((n_buf * tokens, groups * tokens), F32)],
+        scratch_shapes=[pltpu.VMEM((n_buf * tokens, groups * tokens), F32)] + more_scratch,
         cost_estimate=pl.CostEstimate(
             flops=elements * 512, bytes_accessed=n_buf * rows * 512 + groups * rows * 1024, transcendentals=elements
         ),
         compiler_params=pltpu.CompilerParams(vmem_limit_bytes=VMEM_LIMIT),
-    )(*qs, *qids, *bufs, *flat_carry)
+    )(*first_args, *qs, *qids, *bufs, *flat_carry)
     if last:
         return out
     return [(out[2 * g], out[2 * g + 1]) for g in range(groups)]
 
 
-def place_kernel(core_ref, o_mine, o_back, out_ref):
+def place_kernel(core_ref, o_back, half_done, out_ref, sems):
     tokens = out_ref.shape[0]
-    half = out_ref.shape[1] // 2
-    heads = half // HD
-    core = core_ref[0]
-    for side in range(2):
-        @pl.when(core == side)
-        def _():
-            for head in range(heads):
-                rows = slice(head * tokens, (head + 1) * tokens)
-                a = side * half + head * HD
-                b = (1 - side) * half + head * HD
-                out_ref[:, a : a + HD] = o_mine[rows, :]
-                out_ref[:, b : b + HD] = o_back[rows, :]
-
-
-def place(core, o_mine, o_back, tokens, width):
-    vmem = pl.BlockSpec(memory_space=pltpu.VMEM)
+    heads = o_back.shape[0] // tokens
+    other = 1 - core_ref[0]
+    copies = [
+        put_head(o_back, slice(head * tokens, (head + 1) * tokens), out_ref, other, head, sems) for head in range(heads)
+    ]
+    for copy in copies:
+        copy.wait()
+
+
+def place(core, o_back, half_done):
+    hbm = pl.BlockSpec(memory_space=pltpu.HBM)
     return pl.pallas_call(
         place_kernel,
-        in_specs=[pl.BlockSpec(memory_space=pltpu.SMEM), vmem, vmem],
-        out_specs=vmem,
-        out_shape=jax.ShapeDtypeStruct((tokens, width), BF16),
+        in_specs=[pl.BlockSpec(memory_space=pltpu.SMEM), pl.BlockSpec(memory_space=pltpu.VMEM), hbm],
+        out_specs=hbm,
+        out_shape=jax.ShapeDtypeStruct(half_done.shape, BF16),
+        scratch_shapes=[pltpu.SemaphoreType.DMA((o_back.shape[0] // half_done.shape[0],))],
+        input_output_aliases={2: 0},
         compiler_params=pltpu.CompilerParams(vmem_limit_bytes=VMEM_LIMIT),
         name="place",
-    )(core, o_mine, o_back)
+    )(core, o_back, half_done)
 
 
 def layer(queries, key_feats, value_feats, segment_ids):
@@ -258,10 +278,11 @@
     a2x = pair_a(b1x)
     carry = attend(heads, qs, qids, [kv, kvq2, a1, b1], [], False)
     carry = attend(heads, qs, qids, [a1x, b1x, a2, b2], carry, False)
-    (o_other,) = attend(heads, [kvq2], [kvq2], [a2x, b2x], [carry[1]], True)
+    carry = attend(heads, qs, qids, [a2x], carry, False)
+    (o_other,) = attend(heads, [kvq2], [kvq2], [b2x], [carry[1]], True)
     back = swap(o_other)
-    (o_mine,) = attend(heads, [q], [kv], [a2x, b2x], [carry[0]], True)
-    return place(core_arr, o_mine, back, tokens, width)
+    (half_done,) = attend(heads, [q], [kv], [b2x], [carry[0]], True, core_arr)
+    return place(core_arr, back, half_done)
 
 
 def solution(mesh):

time: 79 us -> 82 us (1.038)
  the two profiles are of different devices: /device:TPU:15 before, /device:TPU:13 now
where the time goes in v4:
time: 82 us; the launch traced here: 81.5 us
  starting transfers between devices  52.1 us (64%)
  Pallas kernels  16.7 us (20%)
  waiting for transfers between devices  12.6 us (15%)
    ppermute x4, starting transfers between devices, pair_b(): return lax.ppermute(x, AXES, ups + [(v, u) for u, v in ups])  36.6 us
    pallas_call x5, Pallas kernels, attend(): pl.pallas_call(functools.partial(attend_kernel, heads, tokens, groups, n_...  12.1 us
    ppermute x4, waiting for transfers between devices, pair_a(): return lax.ppermute(x, AXES, [(d, d ^ 2 ^ cross) for d in range(count)])  10.1 us
    ppermute x4, starting transfers between devices, pair_a(): return lax.ppermute(x, AXES, [(d, d ^ 2 ^ cross) for d in range(count)])  9.77 us
    ppermute x2, starting transfers between devices, swap(): return lax.ppermute(x, AXES, [(d, d ^ 1) for d in range(count)])  5.64 us
    pallas_call x2, Pallas kernels, call(): pl.pallas_call(kernel, in_specs=[pl.BlockSpec(memory_space=pltpu.SMEM)] +...  3.82 us
    ppermute x4, waiting for transfers between devices, pair_b(): return lax.ppermute(x, AXES, ups + [(v, u) for u, v in ups])  2.47 us
  transfers between devices with their start and end apart: 10, of which 4 were waited for; matrix products, arithmetic and copies ran while one was open for 0% of the time, Pallas kernels for 15%

profile of v4, /device:TPU:13, one launch (start us, length us, event | category | flops | bytes accessed | tf_op | source)
XLA Modules:
  0.0 81.5 jit_solution(8143850924535701827)
XLA Ops:
  0.0 1.6 %shard_map.46.refs_2_.refs_4_ = bf16[2064,128]{1,0:T(8,128)(2,1)S(1)} custom-call(s32[1]{0:T(128)} %bitcast.core_ref.refs_0_, bf16[128,2048]{1,0:T(8,128)(2,1)} %k_hbm.2, bf16[128,2048]{1,0:T(8,128)(2,1)} %v_hbm.2, s32[1,128]{1,0:T(1,128)} %bitcast.2), custom_call_target="tpu_custom_call" | custom-call | tf_op jit(solution)/shard_map/pallas_call | solution.py:92
  1.7 21.6 %collective-permute-start.5 = (bf16[2064,128]{1,0:T(8,128)(2,1)S(1)}, bf16[2064,128]{1,0:T(8,128)(2,1)S(1)}, u32[]{:S(2)}, u32[]{:S(2)}) collective-permute-start(bf16[2064,128]{1,0:T(8,128)(2,1)S(1)} %shard_map.46.refs_2_.refs_4_), channel_id=1, source_target_pairs={{2,4},{3,5},{6,8},{7,9},{10,12},{11,13},{14,16},{15,17},{18,20},{1... | collective-permute-start | bytes 1585160 | tf_op jit(solution)/shard_map/ppermute | solution.py:265
  23.3 1.9 %collective-permute-start.7 = (bf16[2064,128]{1,0:T(8,128)(2,1)S(1)}, bf16[2064,128]{1,0:T(8,128)(2,1)S(1)}, u32[]{:S(2)}, u32[]{:S(2)}) collective-permute-start(bf16[2064,128]{1,0:T(8,128)(2,1)S(1)} %shard_map.46.refs_2_.refs_4_), channel_id=1, source_target_pairs={{0,2},{1,3},{2,0},{3,1},{4,6},{5,7},{6,4},{7,5},{8,10},{9,11},{10,... | collective-permute-start | bytes 1585160 | tf_op jit(solution)/shard_map/ppermute | solution.py:261
  25.2 2.2 %shard_map.47 = (bf16[2064,128]{1,0:T(8,128)(2,1)S(1)}, bf16[3088,128]{1,0:T(8,128)(2,1)S(1)}, bf16[1024,128]{1,0:T(8,128)(2,1)S(1)}) custom-call(s32[1]{0:T(128)} %bitcast.core_ref.refs_0_, bf16[128,2048]{1,0:T(8,128)(2,1)} %k_hbm.2, bf16[128,2048]{1,0:T(8,128)(2,1)} %v_hbm.2, bf16[128,2048]{1,0:T(8,128)(2,1)} %q_hbm, s32[1,128]{1,0:T(1,128)} %bitcast.3), custom_call_target="tpu_custom_call" | custom-call | tf_op jit(solution)/shard_map/pallas_call | solution.py:92
  27.4 2.5 %collective-permute-start.3 = (bf16[2064,128]{1,0:T(8,128)(2,1)S(1)}, bf16[2064,128]{1,0:T(8,128)(2,1)S(1)}, u32[]{:S(2)}, u32[]{:S(2)}) collective-permute-start(bf16[2064,128]{1,0:T(8,128)(2,1)S(1)} %get-tuple-element.28), channel_id=1, source_target_pairs={{2,5},{3,4},{6,9},{7,8},{10,13},{11,12},{14,17},{15,16},{18,21},{1... | collective-permute-start | bytes 1585160 | tf_op jit(solution)/shard_map/ppermute | solution.py:265
  29.9 3.9 %collective-permute-start.1 = (bf16[2064,128]{1,0:T(8,128)(2,1)S(1)}, bf16[2064,128]{1,0:T(8,128)(2,1)S(1)}, u32[]{:S(2)}, u32[]{:S(2)}) collective-permute-start(bf16[2064,128]{1,0:T(8,128)(2,1)S(1)} %get-tuple-element.28), channel_id=1, source_target_pairs={{0,3},{1,2},{2,1},{3,0},{4,7},{5,6},{6,5},{7,4},{8,11},{9,10},{10,... | collective-permute-start | bytes 1585160 | tf_op jit(solution)/shard_map/ppermute | solution.py:261
  33.8 1.9 %collective-permute-start = (bf16[3088,128]{1,0:T(8,128)(2,1)S(1)}, bf16[3088,128]{1,0:T(8,128)(2,1)S(1)}, u32[]{:S(2)}, u32[]{:S(2)}) collective-permute-start(bf16[3088,128]{1,0:T(8,128)(2,1)S(1)} %get-tuple-element.27), channel_id=1, source_target_pairs={{0,1},{1,0},{2,3},{3,2},{4,5},{5,4},{6,7},{7,6},{8,9},{9,8},{10,11... | collective-permute-start | bytes 2371592 | tf_op jit(solution)/shard_map/ppermute | solution.py:258
  35.7 0.0 collective-permute-done.5.refs_7_
  35.7 2.0 %collective-permute-start.6 = (bf16[2064,128]{1,0:T(8,128)(2,1)S(1)}, bf16[2064,128]{1,0:T(8,128)(2,1)S(1)}, u32[]{:S(2)}, u32[]{:S(2)}) collective-permute-start(bf16[2064,128]{1,0:T(8,128)(2,1)S(1)} %collective-permute-done.5.refs_7_), channel_id=1, source_target_pairs={{0,2},{1,3},{2,0},{3,1},{4,6},{5,7},{6,4},{7,5},{8,10},{9,11},{10,... | collective-permute-start | bytes 1585160 | tf_op jit(solution)/shard_map/ppermute | solution.py:261
  37.8 0.0 collective-permute-done.7.refs_6_
  37.8 7.6 %collective-permute-start.8 = (bf16[2064,128]{1,0:T(8,128)(2,1)S(1)}, bf16[2064,128]{1,0:T(8,128)(2,1)S(1)}, u32[]{:S(2)}, u32[]{:S(2)}) collective-permute-start(bf16[2064,128]{1,0:T(8,128)(2,1)S(1)} %collective-permute-done.7.refs_6_), channel_id=1, source_target_pairs={{2,4},{3,5},{6,8},{7,9},{10,12},{11,13},{14,16},{15,17},{18,20},{1... | collective-permute-start | bytes 1585160 | tf_op jit(solution)/shard_map/ppermute | solution.py:265
  45.4 2.5 %collective-permute-done.3.refs_5_ = bf16[2064,128]{1,0:T(8,128)(2,1)S(1)} collective-permute-done((bf16[2064,128]{1,0:T(8,128)(2,1)S(1)}, bf16[2064,128]{1,0:T(8,128)(2,1)S(1)}, u32[]{:S(2)}, u32[]{:S(2)}) %collective-permute-start.3) | collective-permute-done | bytes 528416 | tf_op jit(solution)/shard_map/ppermute | solution.py:265
  47.8 1.9 %collective-permute-start.4 = (bf16[2064,128]{1,0:T(8,128)(2,1)S(1)}, bf16[2064,128]{1,0:T(8,128)(2,1)S(1)}, u32[]{:S(2)}, u32[]{:S(2)}) collective-permute-start(bf16[2064,128]{1,0:T(8,128)(2,1)S(1)} %collective-permute-done.3.refs_5_), channel_id=1, source_target_pairs={{0,2},{1,3},{2,0},{3,1},{4,6},{5,7},{6,4},{7,5},{8,10},{9,11},{10,... | collective-permute-start | bytes 1585160 | tf_op jit(solution)/shard_map/ppermute | solution.py:261
  49.7 2.2 %collective-permute-done.1.refs_4_ = bf16[2064,128]{1,0:T(8,128)(2,1)S(1)} collective-permute-done((bf16[2064,128]{1,0:T(8,128)(2,1)S(1)}, bf16[2064,128]{1,0:T(8,128)(2,1)S(1)}, u32[]{:S(2)}, u32[]{:S(2)}) %collective-permute-start.1) | collective-permute-done | bytes 528416 | tf_op jit(solution)/shard_map/ppermute | solution.py:261
  51.9 5.0 %collective-permute-start.2 = (bf16[2064,128]{1,0:T(8,128)(2,1)S(1)}, bf16[2064,128]{1,0:T(8,128)(2,1)S(1)}, u32[]{:S(2)}, u32[]{:S(2)}) collective-permute-start(bf16[2064,128]{1,0:T(8,128)(2,1)S(1)} %collective-permute-done.1.refs_4_), channel_id=1, source_target_pairs={{2,4},{3,5},{6,8},{7,9},{10,12},{11,13},{14,16},{15,17},{18,20},{1... | collective-permute-start | bytes 1585160 | tf_op jit(solution)/shard_map/ppermute | solution.py:265
  56.9 0.0 collective-permute-done.refs_1_.refs_3_.refs_5_.refs_0_
  56.9 3.4 %shard_map.48 = (f32[1024,128]{1,0:T(8,128)S(1)}, f32[16,128]{1,0:T(8,128)S(1)}, f32[1024,128]{1,0:T(8,128)S(1)}, f32[16,128]{1,0:T(8,128)S(1)}) custom-call(bf16[1024,128]{1,0:T(8,128)(2,1)S(1)} %get-tuple-element.29.refs_0_.refs_1_, bf16[3088,128]{1,0:T(8,128)(2,1)S(1)} %collective-permute-done.refs_1_.refs_3_.refs_5_.refs_0_, ...), custom_call_target="tpu_custom_call" | custom-call | flops 536870912 | bytes 4194304 | tf_op jit(solution)/shard_map/pallas_call | solution.py:208
  60.4 0.1 collective-permute-done.6.refs_6_
  60.4 0.0 collective-permute-done.8.refs_7_
  60.4 3.5 %shard_map.49 = (f32[1024,128]{1,0:T(8,128)S(1)}, f32[16,128]{1,0:T(8,128)S(1)}, f32[1024,128]{1,0:T(8,128)S(1)}, f32[16,128]{1,0:T(8,128)S(1)}) custom-call(bf16[1024,128]{1,0:T(8,128)(2,1)S(1)} %get-tuple-element.29.refs_0_.refs_1_, bf16[3088,128]{1,0:T(8,128)(2,1)S(1)} %collective-permute-done.refs_1_.refs_3_.refs_5_.refs_0_, ...), custom_call_target="tpu_custom_call" | custom-call | flops 536870912 | bytes 4194304 | tf_op jit(solution)/shard_map/pallas_call | solution.py:208
  63.9 7.9 %collective-permute-done.4.refs_4_ = bf16[2064,128]{1,0:T(8,128)(2,1)S(1)} collective-permute-done((bf16[2064,128]{1,0:T(8,128)(2,1)S(1)}, bf16[2064,128]{1,0:T(8,128)(2,1)S(1)}, u32[]{:S(2)}, u32[]{:S(2)}) %collective-permute-start.4) | collective-permute-done | bytes 528416 | tf_op jit(solution)/shard_map/ppermute | solution.py:261
  71.7 0.8 %shard_map.50 = (f32[1024,128]{1,0:T(8,128)S(1)}, f32[16,128]{1,0:T(8,128)S(1)}, f32[1024,128]{1,0:T(8,128)S(1)}, f32[16,128]{1,0:T(8,128)S(1)}) custom-call(bf16[1024,128]{1,0:T(8,128)(2,1)S(1)} %get-tuple-element.29.refs_0_.refs_1_, bf16[3088,128]{1,0:T(8,128)(2,1)S(1)} %collective-permute-done.refs_1_.refs_3_.refs_5_.refs_0_, ...), custom_call_target="tpu_custom_call" | custom-call | flops 134217728 | bytes 2621440 | tf_op jit(solution)/shard_map/pallas_call | solution.py:208
  72.6 0.0 collective-permute-done.2.refs_2_.refs_3_
  72.6 1.9 %shard_map.51 = bf16[1024,128]{1,0:T(8,128)(2,1)S(1)} custom-call(bf16[3088,128]{1,0:T(8,128)(2,1)S(1)} %collective-permute-done.refs_1_.refs_3_.refs_5_.refs_0_, bf16[3088,128]{1,0:T(8,128)(2,1)S(1)} %collective-permute-done.refs_1_.refs_3_.refs_5_.refs_0_, bf16[2064,128]{1,0:T(8,128)(2,1)S(1)} %collective-permute-done.2.refs_2_.refs_3_, ...), custom_call_target="tpu_custom_call" | custom-call | flops 67108864 | bytes 1572864 | tf_op jit(solution)/shard_map/pallas_call | solution.py:208
  74.5 3.7 %collective-permute-start.9 = (bf16[1024,128]{1,0:T(8,128)(2,1)S(1)}, bf16[1024,128]{1,0:T(8,128)(2,1)S(1)}, u32[]{:S(2)}, u32[]{:S(2)}) collective-permute-start(bf16[1024,128]{1,0:T(8,128)(2,1)S(1)} %shard_map.51), channel_id=1, source_target_pairs={{0,1},{1,0},{2,3},{3,2},{4,5},{5,4},{6,7},{7,6},{8,9},{9,8},{10,11... | collective-permute-start | bytes 786440 | tf_op jit(solution)/shard_map/ppermute | solution.py:258
  78.2 2.6 %shard_map.52.half_done = bf16[128,2048]{1,0:T(8,128)(2,1)} custom-call(s32[1]{0:T(128)} %bitcast.core_ref.refs_0_, bf16[1024,128]{1,0:T(8,128)(2,1)S(1)} %get-tuple-element.29.refs_0_.refs_1_, bf16[2064,128]{1,0:T(8,128)(2,1)S(1)} %shard_map.46.refs_2_.refs_4_, bf16[2064,128]{1,0:T(8,128)(2,1)S(1)} %collective-permute-done.2.refs_2_.refs_3_, ...), custom_call_target="tpu_custom_call" | custom-call | flops 67108864 | bytes 1572864 | tf_op jit(solution)/shard_map/pallas_call | solution.py:208
  80.8 0.0 collective-permute-done.9.o_back
  80.8 0.8 place.1
Async XLA Ops:
  1.7 34.1 %collective-permute-start.5 = (bf16[2064,128]{1,0:T(8,128)(2,1)S(1)}, bf16[2064,128]{1,0:T(8,128)(2,1)S(1)}, u32[]{:S(2)}, u32[]{:S(2)}) collective-permute-start(bf16[2064,128]{1,0:T(8,128)(2,1)S(1)} %shard_map.46.refs_2_.refs_4_), channel_id=1, source_target_pairs={{2,4},{3,5},{6,8},{7,9},{10,12},{11,13},{14,16},{15,17},{18,20},{1... | collective-permute-start | bytes 1585160 | tf_op jit(solution)/shard_map/ppermute | solution.py:265
  23.3 14.5 %collective-permute-start.7 = (bf16[2064,128]{1,0:T(8,128)(2,1)S(1)}, bf16[2064,128]{1,0:T(8,128)(2,1)S(1)}, u32[]{:S(2)}, u32[]{:S(2)}) collective-permute-start(bf16[2064,128]{1,0:T(8,128)(2,1)S(1)} %shard_map.46.refs_2_.refs_4_), channel_id=1, source_target_pairs={{0,2},{1,3},{2,0},{3,1},{4,6},{5,7},{6,4},{7,5},{8,10},{9,11},{10,... | collective-permute-start | bytes 1585160 | tf_op jit(solution)/shard_map/ppermute | solution.py:261
  27.4 20.5 %collective-permute-start.3 = (bf16[2064,128]{1,0:T(8,128)(2,1)S(1)}, bf16[2064,128]{1,0:T(8,128)(2,1)S(1)}, u32[]{:S(2)}, u32[]{:S(2)}) collective-permute-start(bf16[2064,128]{1,0:T(8,128)(2,1)S(1)} %get-tuple-element.28), channel_id=1, source_target_pairs={{2,5},{3,4},{6,9},{7,8},{10,13},{11,12},{14,17},{15,16},{18,21},{1... | collective-permute-start | bytes 1585160 | tf_op jit(solution)/shard_map/ppermute | solution.py:265
  29.9 22.1 %collective-permute-start.1 = (bf16[2064,128]{1,0:T(8,128)(2,1)S(1)}, bf16[2064,128]{1,0:T(8,128)(2,1)S(1)}, u32[]{:S(2)}, u32[]{:S(2)}) collective-permute-start(bf16[2064,128]{1,0:T(8,128)(2,1)S(1)} %get-tuple-element.28), channel_id=1, source_target_pairs={{0,3},{1,2},{2,1},{3,0},{4,7},{5,6},{6,5},{7,4},{8,11},{9,10},{10,... | collective-permute-start | bytes 1585160 | tf_op jit(solution)/shard_map/ppermute | solution.py:261
  33.8 23.1 %collective-permute-start = (bf16[3088,128]{1,0:T(8,128)(2,1)S(1)}, bf16[3088,128]{1,0:T(8,128)(2,1)S(1)}, u32[]{:S(2)}, u32[]{:S(2)}) collective-permute-start(bf16[3088,128]{1,0:T(8,128)(2,1)S(1)} %get-tuple-element.27), channel_id=1, source_target_pairs={{0,1},{1,0},{2,3},{3,2},{4,5},{5,4},{6,7},{7,6},{8,9},{9,8},{10,11... | collective-permute-start | bytes 2371592 | tf_op jit(solution)/shard_map/ppermute | solution.py:258
  35.7 24.7 %collective-permute-start.6 = (bf16[2064,128]{1,0:T(8,128)(2,1)S(1)}, bf16[2064,128]{1,0:T(8,128)(2,1)S(1)}, u32[]{:S(2)}, u32[]{:S(2)}) collective-permute-start(bf16[2064,128]{1,0:T(8,128)(2,1)S(1)} %collective-permute-done.5.refs_7_), channel_id=1, source_target_pairs={{0,2},{1,3},{2,0},{3,1},{4,6},{5,7},{6,4},{7,5},{8,10},{9,11},{10,... | collective-permute-start | bytes 1585160 | tf_op jit(solution)/shard_map/ppermute | solution.py:261
  37.8 22.6 %collective-permute-start.8 = (bf16[2064,128]{1,0:T(8,128)(2,1)S(1)}, bf16[2064,128]{1,0:T(8,128)(2,1)S(1)}, u32[]{:S(2)}, u32[]{:S(2)}) collective-permute-start(bf16[2064,128]{1,0:T(8,128)(2,1)S(1)} %collective-permute-done.7.refs_6_), channel_id=1, source_target_pairs={{2,4},{3,5},{6,8},{7,9},{10,12},{11,13},{14,16},{15,17},{18,20},{1... | collective-permute-start | bytes 1585160 | tf_op jit(solution)/shard_map/ppermute | solution.py:265
  47.8 23.9 %collective-permute-start.4 = (bf16[2064,128]{1,0:T(8,128)(2,1)S(1)}, bf16[2064,128]{1,0:T(8,128)(2,1)S(1)}, u32[]{:S(2)}, u32[]{:S(2)}) collective-permute-start(bf16[2064,128]{1,0:T(8,128)(2,1)S(1)} %collective-permute-done.3.refs_5_), channel_id=1, source_target_pairs={{0,2},{1,3},{2,0},{3,1},{4,6},{5,7},{6,4},{7,5},{8,10},{9,11},{10,... | collective-permute-start | bytes 1585160 | tf_op jit(solution)/shard_map/ppermute | solution.py:261
  51.9 20.7 %collective-permute-start.2 = (bf16[2064,128]{1,0:T(8,128)(2,1)S(1)}, bf16[2064,128]{1,0:T(8,128)(2,1)S(1)}, u32[]{:S(2)}, u32[]{:S(2)}) collective-permute-start(bf16[2064,128]{1,0:T(8,128)(2,1)S(1)} %collective-permute-done.1.refs_4_), channel_id=1, source_target_pairs={{2,4},{3,5},{6,8},{7,9},{10,12},{11,13},{14,16},{15,17},{18,20},{1... | collective-permute-start | bytes 1585160 | tf_op jit(solution)/shard_map/ppermute | solution.py:265
  74.5 6.3 %collective-permute-start.9 = (bf16[1024,128]{1,0:T(8,128)(2,1)S(1)}, bf16[1024,128]{1,0:T(8,128)(2,1)S(1)}, u32[]{:S(2)}, u32[]{:S(2)}) collective-permute-start(bf16[1024,128]{1,0:T(8,128)(2,1)S(1)} %shard_map.51), channel_id=1, source_target_pairs={{0,1},{1,0},{2,3},{3,2},{4,5},{5,4},{6,7},{7,6},{8,9},{9,8},{10,11... | collective-permute-start | bytes 786440 | tf_op jit(solution)/shard_map/ppermute | solution.py:258
